TPU v7x, 32 devices: a whole 2x2x4 slice. The times are simulated.
32 devices in a mesh: dp: 8 (over y, x, core), seq: 4 (over z).
Axes of the slice: x: 2, y: 2, z: 4, core: 2. Of those that a mesh axis runs over, the one named last changes fastest.
Arguments:
- hidden_in: bfloat16 [8, 2048, 1024], P('dp', 'seq'), may hold values from -6 to 6
- doc_lengths: int32 [8, 8], P('dp'), may hold values from 1 to 1024, 2048 in all within a row
- ln1_gain: float32 [1024], replicated, may hold values from 0.1 to 1.9
- ln1_bias: float32 [1024], replicated, may hold values from -1.75 to 1.75
- ln2_gain: float32 [1024], replicated, may hold values from 0.1 to 1.9
- ln2_bias: float32 [1024], replicated, may hold values from -1.75 to 1.75
- qkv_weight: bfloat16 [1024, 3072], replicated, may hold values from -0.1875 to 0.1875
- qkv_bias: float32 [3072], replicated, may hold values from -1.75 to 1.75
- dense_weight: bfloat16 [1024, 1024], replicated, may hold values from -0.75 to 0.75
- dense_bias: float32 [1024], replicated, may hold values from -1.75 to 1.75
- fc_in_weight: bfloat16 [1024, 4096], replicated, may hold values from -0.1875 to 0.1875
- fc_in_bias: float32 [4096], replicated, may hold values from -1.75 to 1.75
- fc_out_weight: bfloat16 [4096, 1024], replicated, may hold values from -0.09375 to 0.09375
- fc_out_bias: float32 [1024], replicated, may hold values from -1.75 to 1.75
- out_grad: bfloat16 [8, 2048, 1024], P('dp', 'seq'), may hold values from -8 to 8
Outputs:
- hidden_out: bfloat16 [8, 2048, 1024], P('dp', 'seq')
- grad_in: float32 [8, 2048, 1024], P('dp', 'seq')
- grad_ln1_gain: float32 [1024], P(('dp', 'seq'))
- grad_ln1_bias: float32 [1024], P(('dp', 'seq'))
- grad_ln2_gain: float32 [1024], P(('dp', 'seq'))
- grad_ln2_bias: float32 [1024], P(('dp', 'seq'))
- grad_qkv_weight: float32 [1024, 3072], P(('dp', 'seq'))
- grad_qkv_bias: float32 [3072], P(('dp', 'seq'))
- grad_dense_weight: float32 [1024, 1024], P(('dp', 'seq'))
- grad_dense_bias: float32 [1024], P(('dp', 'seq'))
- grad_fc_in_weight: float32 [1024, 4096], P(('dp', 'seq'))
- grad_fc_in_bias: float32 [4096], P(('dp', 'seq'))
- grad_fc_out_weight: float32 [4096, 1024], P(('dp', 'seq'))
- grad_fc_out_bias: float32 [1024], P(('dp', 'seq'))
Inputs may be any that keep to these rules, and one draw needn't show every extreme that they name: `doc_lengths`: each row sums to 2048; its last entry is the padding document.
All inputs are finite; a program needn't handle non-finite values.
Results may differ from a plain program's by a relative error of at most 0.0097.
Values may be sent and summed in bfloat16 or wider, within the bound.
A program may use at most 256 MiB of HBM per device.

v0:
```python
import functools
import math

import jax
import jax.numpy as jnp
from jax import lax
from jax.experimental import pallas as pl
from jax.experimental.pallas import tpu as pltpu
from jax.sharding import PartitionSpec as P

HEADS = 16
HEAD = 64
ROT = 16
DOC_MOST = 1024
EPS = 1e-05
NEG = -1e30
LANES = 128
PAIR = 3 * LANES
BLOCK = 256
F32 = jnp.float32
BF16 = jnp.bfloat16
MIB = 1 << 20
VMEM_MIB = 56


def dot(a, b):
    return lax.dot_general(a, b, (((1,), (0,)), ((), ())), preferred_element_type=F32)


def dot_t(a, b):
    return lax.dot_general(a, b, (((1,), (1,)), ((), ())), preferred_element_type=F32)


def whole(shape):
    return pl.BlockSpec(shape, lambda *_: (0,) * len(shape))


def place(to):
    at = {"dp": lax.axis_index("dp"), "seq": lax.axis_index("seq")}
    if to[0] == "ring":
        at["seq"] = lax.rem(at["seq"] + to[1] + to[2], to[2])
    else:
        at[to[0]] = at[to[0]] ^ to[1]
    return (at["dp"], at["seq"])


def both_ways(targets):
    back = [("ring", -to[1], to[2]) for to in targets if to[0] == "ring"]
    return [place(to) for to in sorted({*targets, *back})]


def greet(devices):
    barrier = pltpu.get_barrier_semaphore()
    for device in devices:
        pl.semaphore_signal(barrier, inc=1, device_id=device, device_id_type=pl.DeviceIdType.MESH)
    pl.semaphore_wait(barrier, len(devices))


def call(kernel, *args, grid, in_specs, out_specs, out_shape, name, flops, nbytes, trans=0, scalars=0, scratch=(), after=(), sends=(), cid=None):
    n, n_out, m = scalars + len(in_specs), len(out_specs), len(sends)

    def body(*refs):
        refs = list(refs)
        ins, _, srcs = refs[:n], refs[n : n + len(after)], refs[n + len(after) :][:m]
        rest = refs[n + len(after) + m :]
        outs, gots, own = rest[:n_out], rest[n_out : n_out + m], rest[n_out + m :]
        if not m:
            kernel(*ins, *outs, *own)
            return
        *own, send_sem, recv_sem = own

        def copy(k):
            _, lo, rows, to = sends[k]
            return pltpu.make_async_remote_copy(
                src_ref=srcs[k].at[pl.ds(lo, rows)],
                dst_ref=gots[k],
                send_sem=send_sem.at[k],
                recv_sem=recv_sem.at[k],
                device_id=place(to),
                device_id_type=pl.DeviceIdType.MESH,
            )

        @pl.when(pl.program_id(0) == 0)
        def _():
            greet(both_ways([to for *_, to in sends]))
            for k in range(m):
                copy(k).start()

        kernel(*ins, *outs, *own)

        @pl.when(pl.program_id(0) == grid[0] - 1)
        def _():
            for k in range(m):
                copy(k).wait()

    hbm = pl.BlockSpec(memory_space=pl.ANY)
    more = dict(collective_id=cid, has_side_effects=True) if m else {}
    sems = [pltpu.SemaphoreType.DMA((m,))] * 2 if m else []
    return pl.pallas_call(
        body,
        grid_spec=pltpu.PrefetchScalarGridSpec(
            num_scalar_prefetch=scalars,
            grid=grid,
            in_specs=[*in_specs, *[hbm] * (len(after) + m)],
            out_specs=[*out_specs, *[hbm] * m],
            scratch_shapes=[*scratch, *sems],
        ),
        out_shape=[*out_shape, *[jax.ShapeDtypeStruct((rows, a.shape[1]), a.dtype) for a, _, rows, _ in sends]],
        compiler_params=pltpu.CompilerParams(vmem_limit_bytes=VMEM_MIB * MIB, **more),
        cost_estimate=pl.CostEstimate(flops=int(flops), bytes_accessed=int(nbytes), transcendentals=int(trans)),
        name=name,
    )(*args, *after, *[a for a, *_ in sends])


def stage_bits(size):
    return [1 << b for b in range(size.bit_length() - 1)]


def stage_order(ndp, nseq, kind):
    dp_bits = [("dp", [b]) for b in stage_bits(ndp)]
    seq_bits = [("seq", [b]) for b in stage_bits(nseq)]
    cycle = [*dp_bits[1:], *seq_bits[:1]]
    kind = min(kind, len(cycle) - 1)
    at = (0, len(cycle) - 1, 1)[kind] if kind else 0
    return dp_bits[:1] + cycle[at:] + cycle[:at] + seq_bits[1:]


def short_order(ndp, nseq):
    dp_bits = stage_bits(ndp)
    return [("dp", dp_bits[:1]), ("dp", dp_bits[1:]), ("seq", stage_bits(nseq))]


def flat_bits(stages):
    return [(axis, bit) for axis, bits in stages for bit in bits]


def source(spot, stages, nseq):
    at = {"dp": lax.axis_index("dp"), "seq": lax.axis_index("seq")}
    bits = flat_bits(stages)
    for k, (axis, bit) in enumerate(bits):
        flag = spot // (1 << (len(bits) - 1 - k)) % 2
        if not (isinstance(flag, int) and flag == 0):
            at[axis] = at[axis] + flag * bit * (1 - 2 * (at[axis] // bit % 2))
    return at["dp"] * nseq + at["seq"]


def fan(bits):
    return [sum(b for k, b in enumerate(bits) if (part >> (len(bits) - 1 - k)) & 1) for part in range(1 << len(bits))]


def combine_kernel(counts, slots, *refs):
    outs = refs[sum(counts) :]
    at = 0
    for n, (k, col) in zip(counts, slots):
        total = refs[at][...].astype(F32)
        for r in refs[at + 1 : at + n]:
            total += r[...].astype(F32)
        outs[k][:, col : col + total.shape[1]] = total.astype(outs[k].dtype)
        at += n


def combine(items, after=(), joined=()):
    steps = 4 if all(rows % 64 == 0 for _, _, rows, _ in items) else 1
    ins, specs, counts, slots, shapes, nbytes = [], [], [], [], [], 0
    for k, (arrays, lo, rows, dtype) in enumerate(items):
        block, cols = rows // steps, arrays[0][0].shape[1]
        arrays = [(a, off) for a, off in arrays if off <= lo < off + a.shape[0]]
        for a, off in arrays:
            ins.append(a)
            specs.append(pl.BlockSpec((block, cols), lambda i, at=(lo - off) // block: (at + i, 0)))
        counts.append(len(arrays))
        if k in joined:
            slots.append((len(shapes) - 1, shapes[-1][1]))
            shapes[-1] = (rows, shapes[-1][1] + cols, dtype)
        else:
            slots.append((len(shapes), 0))
            shapes.append((rows, cols, dtype))
        nbytes += rows * cols * 2 * (len(arrays) + 2)
    return call(
        functools.partial(combine_kernel, counts, slots),
        *ins,
        grid=(steps,),
        in_specs=specs,
        out_specs=[pl.BlockSpec((rows // steps, cols), lambda i: (i, 0)) for rows, cols, _ in shapes],
        out_shape=[jax.ShapeDtypeStruct((rows, cols), dtype) for rows, cols, dtype in shapes],
        name="combine",
        flops=nbytes,
        nbytes=nbytes,
        after=after,
    )


class Halving:
    def __init__(self, send, keep, stages, sizes):
        self.keep, self.stages, self.sizes = keep, list(stages), sizes
        self.rows, self.got, self.ready = keep.shape[0], [], [send]

    def targets(self):
        axis, bits = self.stages[0]
        return [(axis, offset) for offset in fan(bits)[1:]]

    def permute(self):
        for part, (axis, offset) in zip(self.ready, self.targets()):
            self.got.append((lax.ppermute(part, axis, [(i, i ^ offset) for i in range(self.sizes[axis])]), 0))
        self.stages.pop(0)

    def sends(self, lo=0, hi=1, parts=1):
        size = self.ready[0].shape[0] // parts
        return [(a, lo * size, (hi - lo) * size, to) for a, to in zip(self.ready, self.targets())]

    def receive(self, arrays, lo=0, hi=1, parts=1, last=True):
        size = self.ready[0].shape[0] // parts
        self.got += [(a, lo * size) for a in arrays]
        if last:
            self.stages.pop(0)

    def items(self):
        arrays = [(self.keep, 0), *self.got]
        parts = 1 << len(self.stages[0][1])
        self.rows //= parts
        return [(arrays, k * self.rows, self.rows, BF16) for k in range(1, parts)]

    def rest(self):
        arrays = [(self.keep, 0), *self.got]
        return arrays, 0, self.rows, BF16


def advance(sums, after):
    groups = [r.items() for r in sums]
    outs = combine([item for group in groups for item in group], after)
    at = 0
    for r, group in zip(sums, groups):
        r.ready = outs[at : at + len(group)]
        at += len(group)
    return [outs[0]]


def unit_of(x):
    mean = jnp.mean(x, axis=-1, keepdims=True)
    c = x - mean
    inv = lax.rsqrt(jnp.mean(c * c, axis=-1, keepdims=True) + EPS)
    return c * inv, inv


def norm_kernel(x_ref, dy_ref, live_ref, g1, b1, g2, b2, a_ref, m_ref, grad_ref, sum_ref):
    u, _ = unit_of(x_ref[...].astype(F32))
    a_ref[...] = (u * g1[...] + b1[...]).astype(BF16)
    m_ref[...] = (u * g2[...] + b2[...]).astype(BF16)
    grad = dy_ref[...].astype(F32) * live_ref[...]
    grad_ref[...] = grad.astype(BF16)

    @pl.when(pl.program_id(0) == 0)
    def _():
        sum_ref[...] = jnp.zeros_like(sum_ref)

    sum_ref[...] += jnp.sum(grad, axis=0, keepdims=True)


def norms(x, dy, live, g1, b1, g2, b2, after=()):
    rows, d = x.shape
    tr = 128
    row = pl.BlockSpec((tr, d), lambda i: (i, 0))
    return call(
        norm_kernel,
        x, dy, live, g1, b1, g2, b2,
        grid=(rows // tr,),
        in_specs=[row, row, pl.BlockSpec((tr, 1), lambda i: (i, 0))] + [whole((1, d))] * 4,
        out_specs=[row, row, row, whole((1, d))],
        out_shape=[jax.ShapeDtypeStruct((rows, d), BF16)] * 3 + [jax.ShapeDtypeStruct((1, d), F32)],
        flops=rows * d * 20, nbytes=rows * d * 10,
        name="norms",
        after=after,
    )


def mlp_kernel(m_ref, grad_ref, win_ref, bin_ref, wout_ref, out_ref, act_ref, dpre_ref, dm_ref, bsum_ref):
    pre = dot(m_ref[...], win_ref[...]) + bin_ref[...]
    cdf = 0.5 * (1.0 + lax.erf(pre * math.sqrt(0.5)))
    act = (pre * cdf).astype(BF16)
    act_ref[...] = act
    d_act = dot_t(grad_ref[...], wout_ref[...])
    slope = cdf + pre * (jnp.exp(-0.5 * pre * pre) * (1.0 / math.sqrt(2.0 * math.pi)))
    d_pre = (d_act * slope).astype(BF16)
    dpre_ref[...] = d_pre
    bsum_ref[...] = jnp.sum(d_pre.astype(F32), axis=0, keepdims=True)

    @pl.when(pl.program_id(0) == 0)
    def _():
        out_ref[...] = jnp.zeros_like(out_ref)
        dm_ref[...] = jnp.zeros_like(dm_ref)

    out_ref[...] += dot(act, wout_ref[...])
    dm_ref[...] += dot_t(d_pre, win_ref[...])


def mlp(m, grad, win, b_in, wout, after=(), sends=(), cid=None):
    rows, d = m.shape
    ff = win.shape[1]
    tf = 512
    cols = pl.BlockSpec((rows, tf), lambda i: (0, i))
    line = pl.BlockSpec((1, tf), lambda i: (0, i))
    return call(
        mlp_kernel,
        m, grad, win, b_in, wout,
        grid=(ff // tf,),
        in_specs=[
            whole((rows, d)),
            whole((rows, d)),
            pl.BlockSpec((d, tf), lambda i: (0, i)),
            line,
            pl.BlockSpec((tf, d), lambda i: (i, 0)),
        ],
        out_specs=[whole((rows, d)), cols, cols, whole((rows, d)), line],
        out_shape=[
            jax.ShapeDtypeStruct((rows, d), F32),
            jax.ShapeDtypeStruct((rows, ff), BF16),
            jax.ShapeDtypeStruct((rows, ff), BF16),
            jax.ShapeDtypeStruct((rows, d), F32),
            jax.ShapeDtypeStruct((1, ff), F32),
        ],
        flops=8 * rows * d * ff, nbytes=4 * d * ff + 4 * rows * ff + 12 * rows * d, trans=rows * ff * 2,
        name="mlp",
        after=after,
        sends=sends,
        cid=cid,
    )


def turned(left, nat_ref, at):
    n = min(BLOCK, left.shape[1])
    eye = lax.broadcasted_iota(jnp.int32, (n, n), 0) == lax.broadcasted_iota(jnp.int32, (n, n), 1)
    eye = jnp.where(eye, 1.0, 0.0).astype(BF16)
    for c in range(0, left.shape[1], n):
        nat_ref[at + c : at + c + n, :] = dot_t(eye, left[:, c : c + n])


def placed(order, nat_ref, lt_ref):
    blocks = 1 << len(flat_bits(order[0]))
    size = nat_ref.shape[0] // blocks
    for b in range(blocks):
        rows = pl.ds(pl.multiple_of(source(b, *order) * size, size), size)
        lt_ref[b * size : (b + 1) * size, :] = nat_ref[rows, :].astype(BF16)


def wgrad_kernel(stacked, orders, steps, starts, per, *refs):
    n = len(starts)
    n_right = -(-sum(steps) // per)
    n_left = len(refs) - n_right - 3 * n - 2
    lefts, rights, refs = refs[:n_left], refs[n_left : n_left + n_right], refs[n_left + n_right :]
    outs, (nat_ref, lt_ref) = refs[:-2], refs[-2:]
    i = pl.program_id(0)

    @pl.when(i == 0)
    def _():
        row = col = 0
        for left in lefts:
            toks, width = left.shape
            turned(left[...], nat_ref.at[:, col : col + toks], row)
            if stacked:
                col += toks
            else:
                row += width

    for g in range(n):
        send_ref, keep_ref, bsum_ref = outs[3 * g : 3 * g + 3]

        @pl.when(i == starts[g])
        def _():
            placed(orders[g], nat_ref, lt_ref)

        for k, right_ref in enumerate(rights):
            first, end = max(starts[g], k * per), min(starts[g] + steps[g], (k + 1) * per)

            @pl.when((i >= first) & (i < end))
            def _():
                half = keep_ref.shape[0]
                right = right_ref[...]
                send_ref[...] = dot(lt_ref[half:, :], right).astype(BF16)
                keep_ref[...] = dot(lt_ref[:half, :], right).astype(BF16)
                bsum_ref[...] = jnp.sum(right.astype(F32), axis=0, keepdims=True)


def wgrad(groups, lefts, right, tn=512, after=(), sends=(), cid=None):
    rights = right if isinstance(right, list) else [right]
    toks, width = rights[0].shape
    stacked = lefts[0].shape[0] < toks
    per = width // tn
    d = lefts[0].shape[1] if stacked else sum(left.shape[1] for left in lefts)
    steps = [cols // tn for _, cols in groups]
    starts = [sum(steps[:g]) for g in range(len(groups))]
    out_specs, out_shape = [], []
    for (_, cols), first, n in zip(groups, starts, steps):
        at = lambda i, *_, first=first, n=n: (0, jnp.clip(i - first, 0, n - 1))
        out_specs += [pl.BlockSpec((d // 2, tn), at)] * 2 + [pl.BlockSpec((1, tn), at)]
        out_shape += [jax.ShapeDtypeStruct((d // 2, cols), BF16)] * 2 + [jax.ShapeDtypeStruct((1, cols), F32)]
    cols = sum(r.shape[1] for r in rights)
    return call(
        functools.partial(wgrad_kernel, stacked, [o for o, _ in groups], steps, starts, per if len(rights) > 1 else sum(steps)),
        *lefts,
        *rights,
        grid=(sum(steps),),
        in_specs=[
            *[whole(left.shape) for left in lefts],
            *[pl.BlockSpec((toks, tn), lambda i, *_, k=k: (0, jnp.clip(i - k * per, 0, per - 1))) for k in range(len(rights))],
        ],
        out_specs=out_specs,
        scratch=[pltpu.VMEM((d, toks), F32), pltpu.VMEM((d, toks), BF16)],
        out_shape=out_shape,
        flops=2 * toks * d * cols,
        nbytes=2 * toks * (d + cols) + 2 * d * cols,
        name="wgrad",
        after=after,
        sends=sends,
        cid=cid,
    )


def wgrad_rows_kernel(turns_n, orders, groups, *refs):
    n = len(groups)
    (left_ref, right_ref), refs = refs[:2], refs[2:]
    outs, (nat_ref, lt_ref) = refs[: 2 * n], refs[2 * n :]
    i = pl.program_id(0)
    tile = left_ref.shape[1]

    @pl.when(i < turns_n)
    def _():
        turned(left_ref[...], nat_ref, 0)
        lt_ref[pl.ds(pl.multiple_of(i * tile, tile), tile), :] = nat_ref[...].astype(lt_ref.dtype)

    for g, (first, steps, lo, cols) in enumerate(groups):
        send_ref, keep_ref = outs[2 * g : 2 * g + 2]
        rows = send_ref.shape[0]

        @pl.when((i >= first) & (i < first + steps))
        def _():
            total = 1 << len(flat_bits(orders[g][0]))
            blocks = total // steps
            size = rows // blocks
            for b in range(blocks):
                spot = ((i - first) * blocks + b + total // 2) % total
                at = pl.ds(pl.multiple_of(source(spot, *orders[g]) * size, size), size)
                nat_ref[b * size : (b + 1) * size, :] = lt_ref[at, :].astype(F32)
            out = dot(nat_ref[:rows, :].astype(BF16), right_ref[:, lo : lo + cols]).astype(BF16)

            @pl.when(i < first + steps // 2)
            def _():
                send_ref[...] = out

            @pl.when(i >= first + steps // 2)
            def _():
                keep_ref[...] = out


def wgrad_rows(groups, left, right, tile=1024, after=(), sends=(), cid=None):
    toks, d = right.shape
    rows = left.shape[1]
    n = rows // tile
    half = n // 2
    orders = [o for o, _ in groups]
    kind = BF16 if (rows >> len(flat_bits(orders[0][0]))) % 16 == 0 else F32
    cuts, out_specs, out_shape, lo = [], [], [], 0
    for g, (_, cols) in enumerate(groups):
        first = n * (g + 1)
        cuts.append((first, n, lo, cols))
        lo += cols
        out_specs.append(pl.BlockSpec((tile, cols), lambda i, *_, first=first: (jnp.clip(i - first, 0, half - 1), 0)))
        out_specs.append(pl.BlockSpec((tile, cols), lambda i, *_, first=first: (jnp.clip(i - first - half, 0, half - 1), 0)))
        out_shape += [jax.ShapeDtypeStruct((rows // 2, cols), BF16)] * 2
    return call(
        functools.partial(wgrad_rows_kernel, n, orders, cuts),
        left,
        right,
        grid=(n * (1 + len(groups)),),
        in_specs=[
            pl.BlockSpec((toks, tile), lambda i, *_: (0, jnp.minimum(i, n - 1))),
            pl.BlockSpec((toks, d), lambda i, *_: (0, 0)),
        ],
        out_specs=out_specs,
        scratch=[pltpu.VMEM((tile, toks), F32), pltpu.VMEM((rows, toks), kind)],
        out_shape=out_shape,
        flops=2 * toks * rows * d,
        nbytes=2 * (rows * (d + toks) + toks * d),
        name="wgrad_rows",
        after=after,
        sends=sends,
        cid=cid,
    )


def d_ctx_kernel(a_ref, w_ref, out_ref):
    out_ref[...] = dot_t(a_ref[...], w_ref[...]).astype(BF16)


def d_context(grad, w, tn=256, after=(), sends=(), cid=None):
    rows, d = grad.shape
    return call(
        d_ctx_kernel,
        grad, w,
        grid=(d // tn,),
        in_specs=[whole((rows, d)), pl.BlockSpec((tn, d), lambda i: (i, 0))],
        out_specs=[pl.BlockSpec((rows, tn), lambda i: (0, i))],
        out_shape=[jax.ShapeDtypeStruct((rows, d), BF16)],
        flops=2 * rows * d * d, nbytes=2 * d * (2 * rows + d),
        name="d_ctx",
        after=after,
        sends=sends,
        cid=cid,
    )


def lane_ids(rows):
    return lax.broadcasted_iota(jnp.int32, (rows, LANES), 1)


def turns():
    frm = lax.broadcasted_iota(jnp.int32, (LANES, LANES), 0)
    to = lax.broadcasted_iota(jnp.int32, (LANES, LANES), 1)
    half = ROT // 2
    within = frm % HEAD
    partner = jnp.where(within < half, frm + half, frm - half)
    rotated = within < ROT
    turned = (frm + HEAD) % LANES
    one = lambda hit: jnp.where(hit, 1.0, 0.0).astype(BF16)
    return one(turned == to), one(rotated & (partner == to)), one(rotated & ((partner + HEAD) % LANES == to))


def split(x):
    high = x.astype(BF16)
    return jnp.concatenate([high, (x - high.astype(F32)).astype(BF16)], axis=1)


def qkv_kernel(n, *refs):
    a_refs, (w_ref, bias_ref, cos_ref, sin_ref, q_ref, k_ref, v_ref) = refs[:n], refs[n:]
    turn, swap, swap_turn = turns()
    k_moves = jnp.concatenate([turn, swap_turn], axis=1)
    k_moves = jnp.concatenate([k_moves, k_moves], axis=0)
    q_moves = jnp.concatenate([swap, swap], axis=0)
    r = 0
    for a_ref in a_refs:
        rows = slice(r, r + a_ref.shape[0])
        r += a_ref.shape[0]
        first = lane_ids(a_ref.shape[0]) < HEAD
        packed = dot(a_ref[...], w_ref[...]) + bias_ref[...]
        cos, sin = cos_ref[rows, :], sin_ref[rows, :]
        for g in range(w_ref.shape[1] // PAIR):
            c = g * PAIR
            lanes = slice(g * LANES, (g + 1) * LANES)
            pa, pb, pc = packed[:, c : c + LANES], packed[:, c + LANES : c + 2 * LANES], packed[:, c + 2 * LANES : c + PAIR]
            both = dot(split(jnp.where(first, pc, pa)), k_moves)
            k_ref[rows, lanes] = (both[:, :LANES] * cos + both[:, LANES:] * sin).astype(BF16)
            v_ref[rows, lanes] = jnp.where(first, pb, pc).astype(BF16)
            if a_ref is a_refs[-1]:
                q = jnp.where(first, pa, pb)
                q_ref[:, lanes] = (q * cos + dot(split(q), q_moves) * sin).astype(BF16)


def qkv(pieces, w, bias, cos, sin, group=4, after=()):
    toks, d = pieces[-1].shape
    win = sum(p.shape[0] for p in pieces)
    cols = w.shape[1]
    out = pl.BlockSpec((win, group * LANES), lambda i: (0, i))
    return call(
        functools.partial(qkv_kernel, len(pieces)),
        *pieces, w, bias, cos, sin,
        grid=(cols // PAIR // group,),
        in_specs=[
            *[whole(p.shape) for p in pieces],
            pl.BlockSpec((d, group * PAIR), lambda i: (0, i)),
            pl.BlockSpec((1, group * PAIR), lambda i: (0, i)),
            whole((win, LANES)),
            whole((win, LANES)),
        ],
        out_specs=[pl.BlockSpec((toks, group * LANES), lambda i: (0, i)), out, out],
        out_shape=[jax.ShapeDtypeStruct((toks, cols // 3), BF16)] + [jax.ShapeDtypeStruct((win, cols // 3), BF16)] * 2,
        flops=2 * win * d * cols, nbytes=8 * win * d + 2 * d * cols,
        name="qkv",
        after=after,
    )


GROUP = 2
QB = 256


def attention_kernel(
    toks, win, start_ref, q_ref, k_ref, v_ref, do_ref, cos_ref, sin_ref, ctx_ref, dp_ref,
    k2, v2, kt, vt, s_ref, e_ref, dq_acc, dk_acc, dv_acc,
):
    nk = win // BLOCK
    halo = win - toks
    first = lane_ids(BLOCK) < HEAD
    first_q = lane_ids(QB) < HEAD
    zero = jnp.zeros((BLOCK, LANES), BF16)
    zero_q = jnp.zeros((QB, LANES), BF16)
    top = lax.broadcasted_iota(jnp.int32, (LANES, QB), 0) < HEAD
    groups = range(GROUP)
    lanes = [slice(g * LANES, (g + 1) * LANES) for g in groups]
    eye = lax.broadcasted_iota(jnp.int32, (LANES, LANES), 0) == lax.broadcasted_iota(jnp.int32, (LANES, LANES), 1)
    upper = lax.broadcasted_iota(jnp.int32, (LANES, LANES), 0) < HEAD
    eye0 = jnp.where(eye & upper, 1.0, 0.0).astype(BF16)
    eye1 = jnp.where(eye & ~upper, 1.0, 0.0).astype(BF16)

    def prepare(j, _):
        rows = pl.ds(pl.multiple_of(j * BLOCK, BLOCK), BLOCK)
        for g in groups:
            for src, two, tr in ((k_ref, k2, kt), (v_ref, v2, vt)):
                x = src[rows, lanes[g]]
                two[g, j, :BLOCK, :] = jnp.where(first, x, zero)
                two[g, j, BLOCK:, :] = jnp.where(first, zero, x)
                tr[g, j, :, :BLOCK] = dot_t(eye0, x).astype(BF16)
                tr[g, j, :, BLOCK:] = dot_t(eye1, x).astype(BF16)
        return 0

    lax.fori_loop(0, nk, prepare, 0)
    dk_acc[...] = jnp.zeros_like(dk_acc)
    dv_acc[...] = jnp.zeros_like(dv_acc)
    scale = HEAD**-0.5
    for i in range(toks // QB):
        rows = slice(i * QB, (i + 1) * QB)
        last = (halo + (i + 1) * QB) // BLOCK
        low = max(halo + i * QB - DOC_MOST + 1, 0) // BLOCK
        qs = [q_ref[rows, lanes[g]].astype(F32) * scale for g in groups]
        qts = [q.T.astype(BF16) for q in qs]
        qs = [q.astype(BF16) for q in qs]
        q2 = [jnp.concatenate([jnp.where(first_q, q, zero_q), jnp.where(first_q, zero_q, q)], axis=0) for q in qs]
        start = start_ref[:, rows]
        q_at = halo + i * QB + lax.broadcasted_iota(jnp.int32, (1, QB), 1)

        def scores(j, peaks):
            at = j * BLOCK + lax.broadcasted_iota(jnp.int32, (BLOCK, QB), 0)
            ok = (at >= start) & (at <= q_at)
            out = []
            for g in groups:
                s = dot(k2[g, j], qts[g])
                s0 = jnp.where(ok, s[:BLOCK], NEG)
                s1 = jnp.where(ok, s[BLOCK:], NEG)
                s_ref[g, j, :BLOCK, :] = s0
                s_ref[g, j, BLOCK:, :] = s1
                out.append(jnp.maximum(peaks[2 * g], jnp.max(s0, axis=0, keepdims=True)))
                out.append(jnp.maximum(peaks[2 * g + 1], jnp.max(s1, axis=0, keepdims=True)))
            return tuple(out)

        floor = jnp.full((1, QB), NEG, F32)
        peaks = lax.fori_loop(low, last, scores, (floor,) * (2 * GROUP), unroll=True)

        def weigh(j, carry):
            out = []
            for g in groups:
                t0, t1, acc = carry[3 * g : 3 * g + 3]
                e0 = jnp.exp(s_ref[g, j, :BLOCK, :] - peaks[2 * g])
                e1 = jnp.exp(s_ref[g, j, BLOCK:, :] - peaks[2 * g + 1])
                b0, b1 = e0.astype(BF16), e1.astype(BF16)
                e_ref[g, j, :BLOCK, :] = b0
                e_ref[g, j, BLOCK:, :] = b1
                acc = acc + dot(vt[g, j], jnp.concatenate([b0, b1], axis=0))
                out += [t0 + jnp.sum(e0, axis=0, keepdims=True), t1 + jnp.sum(e1, axis=0, keepdims=True), acc]
            return tuple(out)

        none = jnp.zeros((1, QB), F32)
        sums = lax.fori_loop(low, last, weigh, (none, none, jnp.zeros((LANES, QB), F32)) * GROUP, unroll=True)
        do_l, do2, d0, d1 = [], [], [], []
        for g in groups:
            t0, t1, acc = sums[3 * g : 3 * g + 3]
            share = jnp.where(top, 1.0 / t0, 1.0 / t1)
            ctx_t = acc * share
            ctx_ref[rows, lanes[g]] = ctx_t.T.astype(BF16)
            do_t = do_ref[rows, lanes[g]].astype(F32).T * share
            both = do_t * ctx_t
            d0.append(jnp.sum(both[:HEAD], axis=0, keepdims=True))
            d1.append(jnp.sum(both[HEAD:], axis=0, keepdims=True))
            do = do_t.T.astype(BF16)
            do_l.append(do_t.astype(BF16))
            do2.append(jnp.concatenate([jnp.where(first_q, do, zero_q), jnp.where(first_q, zero_q, do)], axis=0))

        def back(j, dqs):
            at = pl.ds(pl.multiple_of(j * BLOCK, BLOCK), BLOCK)
            out = []
            for g in groups:
                dp = dot(v2[g, j], do_l[g])
                e0, e1 = e_ref[g, j, :BLOCK, :], e_ref[g, j, BLOCK:, :]
                ds0 = (e0.astype(F32) * (dp[:BLOCK] - d0[g])).astype(BF16)
                ds1 = (e1.astype(F32) * (dp[BLOCK:] - d1[g])).astype(BF16)
                dv_acc[at, lanes[g]] += dot(jnp.concatenate([e0, e1], axis=1), do2[g])
                dk_acc[at, lanes[g]] += dot(jnp.concatenate([ds0, ds1], axis=1), q2[g])
                out.append(dqs[g] + dot(kt[g, j], jnp.concatenate([ds0, ds1], axis=0)))
            return tuple(out)

        dqs = lax.fori_loop(low, last, back, (jnp.zeros((LANES, QB), F32),) * GROUP, unroll=True)
        for g in groups:
            dq_acc[rows, lanes[g]] = dqs[g].T * scale

    turn, swap, swap_turn = turns()
    for j in range(nk):
        rows = slice(j * BLOCK, (j + 1) * BLOCK)
        cos, sin = cos_ref[rows, :], sin_ref[rows, :]
        for g in groups:
            dk = dk_acc[rows, lanes[g]].astype(BF16)
            dk = dot(dk, turn) * cos - dot(dk, swap_turn) * sin
            dv = dv_acc[rows, lanes[g]]
            if j * BLOCK >= halo:
                own = slice(j * BLOCK - halo, (j + 1) * BLOCK - halo)
                dq = dq_acc[own, lanes[g]]
                dq = dq * cos - dot(dq.astype(BF16), swap) * sin
            else:
                dq = jnp.zeros_like(dk)
            c = g * PAIR
            dp_ref[rows, c : c + LANES] = jnp.where(first, dq, dk).astype(BF16)
            dp_ref[rows, c + LANES : c + 2 * LANES] = jnp.where(first, dv, dq).astype(BF16)
            dp_ref[rows, c + 2 * LANES : c + PAIR] = jnp.where(first, dk, dv).astype(BF16)


def attention(start, q, k, v, d_ctx, cos, sin, pair, pairs, after=(), sends=(), cid=None):
    win, d = k.shape
    toks = d_ctx.shape[0]
    nk = win // BLOCK
    width = GROUP * LANES
    at = pair // GROUP
    own = pl.BlockSpec((toks, width), lambda i: (0, at + i))
    every = pl.BlockSpec((win, width), lambda i: (0, at + i))
    out = pairs * LANES
    return call(
        functools.partial(attention_kernel, toks, win),
        start,
        q,
        k,
        v,
        d_ctx,
        cos,
        sin,
        grid=(pairs // GROUP,),
        in_specs=[whole((1, toks)), own, every, every, own, whole((win, LANES)), whole((win, LANES))],
        out_specs=[pl.BlockSpec((toks, width), lambda i: (0, i)), pl.BlockSpec((win, GROUP * PAIR), lambda i: (0, i))],
        out_shape=[jax.ShapeDtypeStruct((toks, out), BF16), jax.ShapeDtypeStruct((win, 3 * out), BF16)],
        scratch=[
            pltpu.VMEM((GROUP, nk, 2 * BLOCK, LANES), BF16),
            pltpu.VMEM((GROUP, nk, 2 * BLOCK, LANES), BF16),
            pltpu.VMEM((GROUP, nk, LANES, 2 * BLOCK), BF16),
            pltpu.VMEM((GROUP, nk, LANES, 2 * BLOCK), BF16),
            pltpu.VMEM((GROUP, nk, 2 * BLOCK, QB), F32),
            pltpu.VMEM((GROUP, nk, 2 * BLOCK, QB), BF16),
            pltpu.VMEM((toks, width), F32),
            pltpu.VMEM((win, width), F32),
            pltpu.VMEM((win, width), F32),
        ],
        flops=pairs * toks * DOC_MOST * 4 * 6 * LANES,
        nbytes=14 * win * out,
        trans=pairs * 2 * toks * DOC_MOST,
        name="attention",
        after=after,
        sends=sends,
        cid=cid,
    )


def tail_kernel(cfg, *refs):
    ndp, nseq, halos, n_pieces, n_dp, n_ctx, joins, last_c = cfg
    refs = list(refs)
    take = lambda n: [refs.pop(0) for _ in range(n)]
    dp_rows, (w_ref,), dp_cols, pieces, ctxs = take(n_dp), take(1), take(n_dp - 2), take(n_pieces), take(n_ctx)
    grad_ref, x_ref, mlp_ref, d_mlp_ref, wd_ref, bias_ref, g1, g2 = take(8)
    gsum_ref, qsum_ref, isum_ref = take(3)
    left_q, own_q = take(2)
    hidden_ref, grad_in_ref, small = take(3)
    owns = take(3)
    last_gots = [take(len(fan(last_c)) - 1) for _ in owns]
    nat, lt, own_acc, far, far_got = take(5)
    group_bufs = [take(6), take(6), [None, own_q.at[0], None, left_q, *take(2)]]
    bsum_ref, small_got = take(2)
    send_sem, recv_sem = refs
    toks, d = x_ref.shape
    me_dp, me_seq = lax.axis_index("dp"), lax.axis_index("seq")
    dp_bits = stage_bits(ndp)
    core, cross = fan(dp_bits[:1]), fan(dp_bits[1:])
    across = fan(last_c)

    def device(axis, offset):
        return (me_dp ^ offset, me_seq) if axis == "dp" else (me_dp, me_seq ^ offset)

    behind = (me_dp, lax.rem(me_seq + nseq - 1, nseq))
    ahead = (me_dp, lax.rem(me_seq + 1, nseq))
    names = {}

    def copy(name, src, dst, to):
        k = names.setdefault(name, len(names))
        return pltpu.make_async_remote_copy(
            src_ref=src,
            dst_ref=dst,
            send_sem=send_sem.at[k],
            recv_sem=recv_sem.at[k],
            device_id=to,
            device_id_type=pl.DeviceIdType.MESH,
        )

    far_copy = lambda k: copy(("far", k), far.at[k], far_got.at[k], behind)

    def first(n):
        send, _, got, *_ = group_bufs[n]
        return copy(("core", n), send, got, device("dp", core[1]))

    def second(n):
        _, _, _, out, into, _ = group_bufs[n]
        start = 1 if n < 2 else 0
        return [copy(("cross", n, k), out.at[k - start], into.at[k - 1], device("dp", cross[k])) for k in range(1, len(cross))]

    def third(n):
        out, got = group_bufs[n][5], last_gots[(n + 1) % 3]
        return [copy(("across", n, k), out.at[k - 1], got[k - 1], device("seq", across[k])) for k in range(1, len(across))]

    def to_second(n):
        _, keep, got, out, _, _ = group_bufs[n]
        first(n).wait()
        rows = out.shape[1]
        for k, c in enumerate(second(n), 1):
            at = slice(k * rows, (k + 1) * rows)
            out[k - 1] = (keep[at, :].astype(F32) + got[at, :].astype(F32)).astype(BF16)
            c.start()

    def to_third(n):
        _, keep, got, _, into, out = group_bufs[n]
        for c in second(n):
            c.wait()
        own = owns[(n + 1) % 3]
        rows = own.shape[0]
        copies = third(n)
        for k in reversed(range(len(across))):
            at = slice(k * rows, (k + 1) * rows)
            total = keep[at, :].astype(F32)
            if got is not None:
                total += got[at, :].astype(F32)
            for b in range(len(cross) - 1):
                total += into[b, at, :].astype(F32)
            if k:
                out[k - 1] = total.astype(out.dtype)
                copies[k - 1].start()
            else:
                own[...] = total

    def pass_on(k):
        far_copy(k - 1).wait()
        far[k] = (far[k].astype(F32) + far_got[k - 1].astype(F32)).astype(BF16)
        far_copy(k).start()

    def back(cols=None):
        total, at = None, 0
        for a_ref in dp_rows:
            n = a_ref.shape[1]
            term = dot_t(a_ref[...], w_ref[:, at : at + n])
            total, at = term if total is None else total + term, at + n
        return total

    step = [0]
    pid = pl.program_id(0)

    def phase(fn):
        pl.when(pid == step[0])(fn)
        step[0] += 1

    for k in range(halos):

        def do_far(k=k):
            if k == 0:
                offsets = [("dp", o) for o in (*core[1:], *cross[1:])] + [("seq", o) for o in across[1:]]
                greet([device(*o) for o in offsets] + [behind, ahead])
                for c in second(2):
                    c.start()
            far[k] = back().astype(BF16)
            if k == 0:
                far_copy(0).start()

        phase(do_far)

    def do_columns():
        col = 0
        for left in pieces:
            n = left.shape[0]
            turned(left[...], nat.at[:, :n], 0)
            placed((short_order(ndp, nseq), nseq), nat.at[:, :n], lt.at[:, col : col + n])
            col += n
        send, keep = group_bufs[0][:2]
        half, at = keep.shape[0], 0
        for right_ref in dp_cols:
            right = right_ref[...]
            n = right.shape[1]
            send[:, at : at + n] = dot(lt[half:, :], right).astype(BF16)
            keep[:, at : at + n] = dot(lt[:half, :], right).astype(BF16)
            bsum_ref[:, at : at + n] = jnp.sum(right.astype(F32), axis=0, keepdims=True)
            at += n
        first(0).start()

    phase(do_columns)

    def do_dense():
        at = 0
        for ctx in ctxs:
            turned(ctx[...], nat, at)
            at += ctx.shape[1]
        placed((short_order(ndp, nseq), nseq), nat, lt.at[:, :toks])
        send, keep = group_bufs[1][:2]
        half = keep.shape[0]
        send[...] = dot(lt[half:, :toks], grad_ref[...]).astype(BF16)
        first(1).start()
        keep[...] = dot(lt[:half, :toks], grad_ref[...]).astype(BF16)
        to_second(0)
        to_third(2)

    phase(do_dense)

    def do_own():
        own_acc[...] = back()
        to_second(1)

    phase(do_own)
    for t in range(joins):

        def do_join(t=t):
            cols = hidden_ref.shape[1]
            at = slice(t * cols, (t + 1) * cols)
            total, row = x_ref[:, at].astype(F32) + mlp_ref[...] + bias_ref[:, at], 0
            for ctx in ctxs:
                n = ctx.shape[1]
                total += dot(ctx[...], wd_ref[row : row + n, :])
                row += n
            hidden_ref[...] = total.astype(BF16)
            if t == 0 and halos > 1:
                pass_on(1)

        phase(do_join)

    def do_rest():
        for k in range(2, halos):
            pass_on(k)
        to_third(0)
        to_third(1)
        far_copy(halos - 1).wait()
        small[...] = jnp.zeros_like(small)
        rows = min(128, toks)
        for r in range(0, toks, rows):
            at = slice(r, r + rows)
            u, inv = unit_of(x_ref[at, :].astype(F32))
            d1 = own_acc[at, :] + far_got[halos - 1, at, :].astype(F32)
            d2 = d_mlp_ref[at, :]
            e = d1 * g1[...] + d2 * g2[...]
            dx = inv * (e - jnp.mean(e, axis=-1, keepdims=True) - u * jnp.mean(e * u, axis=-1, keepdims=True))
            grad_in_ref[at, :] = grad_ref[at, :].astype(F32) + dx
            for k, v in enumerate((d1 * u, d1, d2 * u, d2)):
                small[k : k + 1, :] += jnp.sum(v, axis=0, keepdims=True)
        small[4:5, :] = gsum_ref[...]
        row = 5
        for parts in ((qsum_ref, bsum_ref), (isum_ref,)):
            flat = jnp.concatenate([p[...] for p in parts], axis=1)
            for c in range(0, flat.shape[1], d):
                small[row : row + 1, :] = flat[:, c : c + d]
                row += 1
        used = 0
        for axis, offsets in (("dp", core), ("dp", cross), ("seq", across)):
            copies = []
            for o in offsets[1:]:
                copies.append(copy(("small", used), small, small_got.at[used], device(axis, o)))
                copies[-1].start()
                used += 1
            for c in copies:
                c.wait()
            total = small[...]
            for k in range(used - len(copies), used):
                total += small_got[k]
            small[...] = total
        for c in third(0) + third(1) + third(2):
            c.wait()

    phase(do_rest)


def tail(dps, w, pieces, ctxs, grad, x, mlp_out, d_mlp, w_d, bias, g1, g2, sums, left_q, ndp, nseq, halos, after=()):
    toks, d = x.shape
    depth = w.shape[1]
    joins = 4
    own_at = halos + 2
    dp_bits, seq_bits = stage_bits(ndp), stage_bits(nseq)
    cross, across = 1 << len(dp_bits[1:]), 1 << len(seq_bits)
    tile = d // joins
    once = lambda shape: pl.BlockSpec(shape, lambda i: (0,) * len(shape), pipeline_mode=pl.Buffered(1))
    piece_at = lambda i: (jnp.where(i < halos, i, jnp.where(i < own_at, halos - 1, halos)), 0)
    join_at = lambda i: (0, jnp.clip(i - own_at - 1, 0, joins - 1))
    hbm = pl.BlockSpec(memory_space=pl.ANY)
    cut_up = lambda a, n: a.reshape(n, a.shape[0] // n, a.shape[1])
    left_q = cut_up(left_q, cross)
    ins = [*dps, w, *dps[2:], *pieces, *ctxs, grad, x, mlp_out, d_mlp, w_d, bias, g1, g2, *sums, left_q, left_q]
    in_specs = (
        [pl.BlockSpec((toks, a.shape[1]), piece_at) for a in dps]
        + [once(w.shape)]
        + [once(a.shape) for a in dps[2:]]
        + [once(p.shape) for p in pieces]
        + [once(c.shape) for c in ctxs]
        + [once((toks, d))] * 2
        + [pl.BlockSpec((toks, tile), join_at), once((toks, d)), pl.BlockSpec((d, tile), join_at)]
        + [once((1, d))] * 3
        + [once(v.shape) for v in sums]
        + [hbm, once((1, *left_q.shape[1:]))]
    )
    rest = sum(a.shape[1] for a in dps[2:])
    lines = 4 + sum(v.shape[1] for v in sums) // d + 1
    lines += -lines % 8
    widths = [left_q.shape[2], rest, d]
    left = d // 2 // cross // across
    kind = BF16 if left % 16 == 0 else F32
    out_shape = [
        jax.ShapeDtypeStruct((toks, d), BF16),
        jax.ShapeDtypeStruct((toks, d), F32),
        jax.ShapeDtypeStruct((lines, d), F32),
        *[jax.ShapeDtypeStruct((left, n), F32) for n in widths],
        *[jax.ShapeDtypeStruct((left, n), kind) for n in widths for _ in range(across - 1)],
    ]
    fixed = lambda shape: pl.BlockSpec(shape, lambda i: (0,) * len(shape))
    out_specs = (
        [pl.BlockSpec((toks, tile), join_at), fixed((toks, d))]
        + [fixed((lines, d))]
        + [fixed((left, n)) for n in widths]
        + [hbm] * (len(widths) * (across - 1))
    )
    scratch = [
        pltpu.VMEM((d, toks), F32),
        pltpu.VMEM((d, toks * (halos + 1)), BF16),
        pltpu.VMEM((toks, d), F32),
        pltpu.VMEM((halos, toks, d), BF16),
        pltpu.VMEM((halos, toks, d), BF16),
    ]
    for n in widths[1:]:
        scratch += [pltpu.VMEM((d // 2, n), BF16)] * 3
        scratch += [pltpu.VMEM((cross - 1, d // 2 // cross, n), BF16)] * 2
        scratch += [pltpu.VMEM((across - 1, left, n), kind)]
    scratch += [pltpu.VMEM((cross - 1, *left_q.shape[1:]), BF16), pltpu.VMEM((across - 1, left, widths[0]), kind)]
    scratch += [pltpu.VMEM((1, rest), F32), pltpu.VMEM((1 + cross - 1 + across - 1, lines, d), F32)]
    copies = halos + 4 * (1 + cross - 1 + across - 1)
    scratch += [pltpu.SemaphoreType.DMA((copies,))] * 2
    cfg = (ndp, nseq, halos, len(pieces), len(dps), len(ctxs), joins, seq_bits)
    n = len(ins)

    def body(*refs):
        tail_kernel(cfg, *refs[:n], *refs[n + len(after) :])

    outs = pl.pallas_call(
        body,
        grid_spec=pltpu.PrefetchScalarGridSpec(
            num_scalar_prefetch=0,
            grid=(own_at + 1 + joins + 1,),
            in_specs=in_specs + [hbm] * len(after),
            out_specs=out_specs,
            scratch_shapes=scratch,
        ),
        out_shape=out_shape,
        compiler_params=pltpu.CompilerParams(vmem_limit_bytes=63 * MIB, collective_id=1, has_side_effects=True),
        cost_estimate=pl.CostEstimate(flops=20 * toks * d * depth, bytes_accessed=40 * toks * d, transcendentals=0),
        name="tail",
    )(*ins, *after)
    outs = list(outs)
    main, own, outs = outs[:3], outs[3:6], outs[6:]
    terms = []
    for a in own:
        terms.append(([(v, 0) for v in (a, *outs[: across - 1])], 0, left, F32))
        outs = outs[across - 1 :]
    return main, terms


def shards(
    hidden_in,
    doc_lengths,
    ln1_gain,
    ln1_bias,
    ln2_gain,
    ln2_bias,
    qkv_weight,
    qkv_bias,
    dense_weight,
    dense_bias,
    fc_in_weight,
    fc_in_bias,
    fc_out_weight,
    fc_out_bias,
    out_grad,
):
    _, toks, d = hidden_in.shape
    ff = fc_in_weight.shape[1]
    ndp, nseq = lax.axis_size("dp"), lax.axis_size("seq")
    ndev = ndp * nseq
    sizes = {"dp": ndp, "seq": nseq}
    me_dp, me_seq = lax.axis_index("dp"), lax.axis_index("seq")
    row = lambda v: v.reshape(1, -1)

    halos = min(-(-(DOC_MOST - 1) // toks), nseq - 1)
    halos = max(halos, 1)
    win = (halos + 1) * toks
    base = (me_seq - halos) * toks
    lengths = doc_lengths.reshape(-1)
    docs = lengths.shape[0]
    doc = jnp.arange(docs, dtype=jnp.int32)
    ends = jnp.sum(jnp.where(doc[None, :] <= doc[:, None], lengths[None, :], 0), axis=1)
    at = base + jnp.arange(win, dtype=jnp.int32)
    begin = jnp.max(jnp.where(at[:, None] >= ends[None, :], ends[None, :], 0), axis=1)
    doc_pos = at - begin
    live = (at[halos * toks :] < ends[docs - 2]).astype(F32).reshape(toks, 1)
    start = (begin - base)[halos * toks :]
    lane = jnp.arange(LANES, dtype=jnp.int32) % HEAD
    half = ROT // 2
    freq = 10000.0 ** (-(2.0 * (lane % half).astype(F32)) / ROT)
    angle = doc_pos.astype(F32)[:, None] * freq[None, :]
    cos = jnp.where(lane < ROT, jnp.cos(angle), 1.0)
    sin = jnp.where(lane < half, -1.0, jnp.where(lane < ROT, 1.0, 0.0)) * jnp.sin(angle)

    x = hidden_in.reshape(toks, d)
    a_own, m_own, grad, grad_sum = norms(
        x, out_grad.reshape(toks, d), live, row(ln1_gain), row(ln1_bias), row(ln2_gain), row(ln2_bias)
    )

    ahead = [(i, (i + 1) % nseq) for i in range(nseq)]
    on = ("ring", 1, nseq)
    mlp_out, act, d_pre, d_mlp, b_in_sum, near = mlp(
        m_own, grad, fc_in_weight, row(fc_in_bias), fc_out_weight, sends=[(a_own, 0, toks, on)], cid=2
    )
    pieces = [a_own, near]

    orders = [stage_order(ndp, nseq, kind) for kind in range(3)]
    srcs = [(o, nseq) for o in orders]
    in_cut, out_cut = ff * 5 // 8, d // 4
    hop = [[(near, k * toks // 2, toks // 2, on)] if halos > 1 else [] for k in range(2)]
    s0, k0, _, s1, k1, _, *far_low = wgrad(
        [(srcs[0], in_cut), (srcs[2], ff - in_cut)], [m_own], d_pre, sends=hop[0], cid=3 if hop[0] else None
    )
    early = [Halving(s0, k0, orders[0], sizes), Halving(s1, k1, orders[2], sizes)]
    s2, k2, s3, k3, *got = wgrad_rows(
        [(srcs[2], out_cut), (srcs[1], d - out_cut)],
        act,
        grad,
        after=far_low,
        sends=[send for r in early for send in r.sends()] + hop[1],
        cid=4,
    )
    for r in early:
        r.receive([got.pop(0)])
    if halos > 1:
        pieces += [got[0], far_low[0]]
    for k in range(2, halos):
        after_two = jnp.concatenate([pieces[3], pieces[2]], axis=0) if k == 2 else pieces[-1]
        pieces.append(lax.ppermute(after_two, "seq", ahead))
    late = [Halving(s2, k2, orders[2], sizes), Halving(s3, k3, orders[1], sizes)]
    fc = early + late
    d_ctx, *got = d_context(grad, dense_weight, sends=[send for r in late for send in r.sends()], cid=5)
    for r in late:
        r.receive([got.pop(0)])
    last = advance(fc, [d_ctx])
    for r in fc:
        r.permute()
    pieces = pieces[::-1]
    q, k, v = qkv(pieces, qkv_weight, row(qkv_bias), cos, sin, after=last)

    order_c = short_order(ndp, nseq)
    src_c = (order_c, nseq)
    pairs = d // LANES
    quarter = pairs // 4

    def part(at, n, sums=(), **more):
        sends = [send for r in sums for send in r.sends()]
        ctx, dp, *got = attention(
            row(start), q, k, v, d_ctx, cos, sin, at * quarter, n * quarter, sends=sends, cid=6 + at if sends else None, **more
        )
        for r in sums:
            r.receive([got.pop(0) for _ in r.targets()])
        return ctx, dp

    ctx_a, dp_a = part(0, 1)
    advance(fc, [ctx_a])
    ctx_b, dp_b = part(1, 1, fc)
    advance(fc, [ctx_b])
    qa_send, qa_keep, b_qkv_a, *got = wgrad(
        [(src_c, dp_a.shape[1] * 2)], pieces, [dp_a, dp_b], tn=dp_a.shape[1], sends=[send for r in fc for send in r.sends()], cid=10
    )
    for r in fc:
        r.receive([got.pop(0) for _ in r.targets()])
    r_qa = Halving(qa_send, qa_keep, order_c, sizes)
    last = advance(fc, [b_qkv_a])
    while len(fc[0].stages) > 1:
        for r in fc:
            r.permute()
        last = advance(fc, last)
    ctx_c, dp_c = part(2, 2, [*fc, r_qa])
    left_q, g_in, g_out = combine([r_qa.rest(), *[(*r.rest()[:3], F32) for r in fc]], [ctx_c], joined=(2, 4))
    main, terms = tail(
        [dp_a, dp_b, dp_c],
        qkv_weight,
        pieces,
        [ctx_a, ctx_b, ctx_c],
        grad,
        x,
        mlp_out,
        d_mlp,
        dense_weight,
        row(dense_bias + fc_out_bias),
        row(ln1_gain),
        row(ln2_gain),
        [grad_sum, b_qkv_a, b_in_sum],
        left_q,
        ndp,
        nseq,
        halos,
    )
    hidden_out, grad_in, small = main
    g_qkv, g_dense = combine(terms, joined=(1,))
    mine = lambda lo, rows: lax.dynamic_slice_in_dim(
        small[lo : lo + rows].reshape(-1), (me_dp * nseq + me_seq) * (rows * d // ndev), rows * d // ndev
    )
    o1g, o1b, o2g, o2b, o_db = (mine(k, 1) for k in range(5))
    o_qb, o_ib = mine(5, 3), mine(8, ff // d)
    return (
        hidden_out.reshape(hidden_in.shape),
        grad_in.reshape(hidden_in.shape),
        o1g,
        o1b,
        o2g,
        o2b,
        g_qkv,
        o_qb,
        g_dense,
        o_db,
        g_in,
        o_ib,
        g_out,
        o_db,
    )


def solution(mesh):
    both = P(("dp", "seq"))
    rows = P(("dp", "seq"), None)
    toks = P("dp", "seq", None)
    return jax.shard_map(
        shards,
        mesh=mesh,
        in_specs=(toks, P("dp", None)) + (P(),) * 12 + (toks,),
        out_specs=(toks, toks, both, both, both, both, rows, both, rows, both, rows, both, rows, both),
        check_vma=False,
    )
```

profile of v0, /device:TPU:0, one launch (start us, length us, event | category | flops | bytes accessed | tf_op | source)
XLA Modules:
  0.0 330.4 jit_solution(12077248281462959275)
XLA Ops:
  0.7 0.8 select_reduce_fusion.1
  1.4 0.6 slice.32
  2.0 0.6 fusion.2
  2.7 0.9 copy.30.refs_2_
  3.5 4.6 %norms.1 = (bf16[512,1024]{1,0:T(8,128)(2,1)}, bf16[512,1024]{1,0:T(8,128)(2,1)}, bf16[512,1024]{1,0:T(8,128)(2,1)}, f32[1,1024]{1,0:T(1,128)}) custom-call(bf16[512,1024]{1,0:T(8,128)(2,1)} %bitcast.33, bf16[512,1024]{1,0:T(8,128)(2,1)} %bitcast.32, f32[512,1]{1,0:T(8,128)} %copy.30.refs_2_, f32[1,1024]{1,0:T(1,128)} %bitcast.43, f32[1,1024]{1,0:T(1,128)} %bitcast.41, ...), custom_call_target="tpu_custom_call" | custom-call | flops 10485760 | bytes 5242880 | tf_op jit(solution)/shard_map/norms/pallas_call | solution.py:99
  8.1 33.7 %mlp.1 = (f32[512,1024]{1,0:T(8,128)}, bf16[512,4096]{1,0:T(8,128)(2,1)}, bf16[512,4096]{1,0:T(8,128)(2,1)}, f32[512,1024]{1,0:T(8,128)}, f32[1,4096]{1,0:T(1,128)}, /*index=5*/bf16[512,1024]{1,0:T(8,128)(2,1)}) custom-call(bf16[512,1024]{1,0:T(8,128)(2,1)} %get-tuple-element.100.refs_0_, bf16[512,1024]{1,0:T(8,128)(2,1)} %get-tuple-element.101.refs_1_.refs_0_.refs_12_, ...), custom_call_target="tpu_custom_call" | custom-call | flops 17179869184 | bytes 31457280 | tf_op jit(solution)/shard_map/mlp/pallas_call | solution.py:99
  41.8 17.8 %wgrad.2 = (bf16[512,2560]{1,0:T(8,128)(2,1)}, bf16[512,2560]{1,0:T(8,128)(2,1)}, f32[1,2560]{1,0:T(1,128)}, bf16[512,1536]{1,0:T(8,128)(2,1)}, bf16[512,1536]{1...) custom-call(bf16[512,1024]{1,0:T(8,128)(2,1)} %get-tuple-element.100.refs_0_, ...), custom_call_target="tpu_custom_call" | custom-call | flops 4294967296 | bytes 13631488 | tf_op jit(solution)/shard_map/wgrad/pallas_call | solution.py:99
  59.6 17.7 %wgrad_rows.1 = (bf16[2048,256]{1,0:T(8,128)(2,1)}, bf16[2048,256]{1,0:T(8,128)(2,1)}, bf16[2048,768]{1,0:T(8,128)(2,1)}, bf16[2048,768]{1,0:T(8,128)(2,1)}, bf1...) custom-call(bf16[512,4096]{1,0:T(8,128)(2,1)} %get-tuple-element.106.refs_0_, ...), custom_call_target="tpu_custom_call" | custom-call | flops 4294967296 | bytes 13631488 | tf_op jit(solution)/shard_map/wgrad_rows/pallas_call | solution.py:99
  77.3 9.7 %d_ctx.1 = (bf16[512,1024]{1,0:T(8,128)(2,1)}, bf16[2048,256]{1,0:T(8,128)(2,1)}, bf16[2048,768]{1,0:T(8,128)(2,1)}) custom-call(bf16[512,1024]{1,0:T(8,128)(2,1)} %get-tuple-element.101.refs_1_.refs_0_.refs_12_, bf16[1024,1024]{1,0:T(8,128)(2,1)} %refs_16_.1, bf16[2048,256]{1,0:T(8,128)(2,1)} %get-tuple-element.115.refs_2_, ...), custom_call_target="tpu_custom_call" | custom-call | flops 1073741824 | bytes 4194304 | tf_op jit(solution)/shard_map/d_ctx/pallas_call | solution.py:99
  87.0 5.9 %combine.6 = (bf16[256,2560]{1,0:T(8,128)(2,1)}, bf16[256,1536]{1,0:T(8,128)(2,1)}, bf16[1024,256]{1,0:T(8,128)(2,1)}, bf16[1024,768]{1,0:T(8,128)(2,1)}) custom-call(bf16[512,2560]{1,0:T(8,128)(2,1)} %get-tuple-element.110.refs_0_.refs_2_, bf16[512,2560]{1,0:T(8,128)(2,1)} %get-tuple-element.111.refs_1_.refs_3_, ...), custom_call_target="tpu_custom_call" | custom-call | flops 16777216 | bytes 16777216 | tf_op jit(solution)/shard_map/combine/pallas_call | solution.py:99
  92.8 1.0 collective-permute-start.3
  93.9 1.5 collective-permute-start
  95.3 1.5 collective-permute-start.1
  96.9 0.5 collective-permute-start.2
  97.4 0.1 select_reduce_fusion
  97.5 4.3 %fusion.1 = (f32[1536,128]{1,0:T(8,128)}, f32[1536,128]{1,0:T(8,128)}) fusion(f32[128]{0:T(128)S(1)} %get-tuple-element.193, f32[128]{0:T(128)S(1)} %get-tuple-element.194, f32[1536]{0:T(1024)S(1)} %subtract_convert_fusion, pred[128]{0:T(512)(128)(4,1)S(1)} %broadcast_compare_fusion), kind=kLoop, calls=%fused_computation.3 | loop fusion | flops 589824 | bytes 1580160 | tf_op jit(solution)/shard_map/mul | solution.py:1107
  101.9 0.0 copy-start.4
  101.9 0.0 copy-start.5
  101.9 17.9 %qkv.1 = (bf16[512,1024]{1,0:T(8,128)(2,1)}, bf16[1536,1024]{1,0:T(8,128)(2,1)}, bf16[1536,1024]{1,0:T(8,128)(2,1)}) custom-call(bf16[256,1024]{1,0:T(8,128)(2,1)} %get-tuple-element.105.refs_2_.refs_0_.refs_5_, bf16[256,1024]{1,0:T(8,128)(2,1)} %get-tuple-element.109.refs_1_.refs_6_, bf16[512,1024]{1,0:T(8,128)(2,1)} %get-tuple-element.104.refs_2_.refs_5_.refs_7_, ...), custom_call_target="tpu_custom_call" | custom-call | flops 9663676416 | bytes 18874368 | tf_op jit(solution)/shard_map/qkv/pallas_call | solution.py:99
  119.7 0.0 copy-done.4
  119.7 0.0 copy-done.5
  119.7 0.6 add.68
  120.3 0.6 slice_subtract_fusion
  120.9 15.4 %attention.3 = (bf16[512,256]{1,0:T(8,128)(2,1)}, bf16[1536,768]{1,0:T(8,128)(2,1)}) custom-call(s32[1,512]{1,0:T(1,128)} %bitcast.37, bf16[512,1024]{1,0:T(8,128)(2,1)} %get-tuple-element.122.refs_1_, bf16[1536,1024]{1,0:T(8,128)(2,1)} %get-tuple-element.123.refs_2_, bf16[1536,1024]{1,0:T(8,128)(2,1)} %get-tuple-element.124.refs_3_, ...), custom_call_target="tpu_custom_call" | custom-call | flops 3221225472 | bytes 5505024 | tf_op jit(solution)/shard_map/attention/pallas_call | solution.py:99
  136.3 0.0 collective-permute-done.2.refs_8_.refs_10_.refs_12_.refs_16_
  136.3 0.0 copy-start.2
  136.3 0.0 collective-permute-done.1.refs_5_.refs_6_.refs_7_.refs_10_
  136.3 0.0 collective-permute-done.refs_2_.refs_4_
  136.3 0.0 copy-start.1
  136.4 0.0 collective-permute-done.3.refs_11_.refs_14_.refs_17_.refs_22_
  136.4 0.0 copy-start
  136.4 0.7 copy-done.2
  137.1 0.4 copy-done.1
  137.6 0.5 copy-done
  138.1 4.8 %combine.7 = (bf16[128,2560]{1,0:T(8,128)(2,1)}, bf16[128,1536]{1,0:T(8,128)(2,1)}, bf16[512,256]{1,0:T(8,128)(2,1)}, bf16[512,768]{1,0:T(8,128)(2,1)}) custom-call(bf16[512,2560]{1,0:T(8,128)(2,1)} %get-tuple-element.110.refs_0_.refs_2_, bf16[512,2560]{1,0:T(8,128)(2,1)} %get-tuple-element.111.refs_1_.refs_3_, bf16[256,2560]{1,0:T(8,128)(2,1)} %copy-done.1, ...), custom_call_target="tpu_custom_call" | custom-call | flops 10485760 | bytes 10485760 | tf_op jit(solution)/shard_map/combine/pallas_call | solution.py:99
  142.9 28.3 %attention.4 = (bf16[512,256]{1,0:T(8,128)(2,1)}, bf16[1536,768]{1,0:T(8,128)(2,1)}, bf16[128,2560]{1,0:T(8,128)(2,1)}, bf16[128,1536]{1,0:T(8,128)(2,1)}, bf16[...) custom-call(s32[1,512]{1,0:T(1,128)} %bitcast.38, bf16[512,1024]{1,0:T(8,128)(2,1)} %get-tuple-element.122.refs_1_, ...), custom_call_target="tpu_custom_call" | custom-call | flops 3221225472 | bytes 5505024 | tf_op jit(solution)/shard_map/attention/pallas_call | solution.py:99
  171.2 4.2 %combine.8 = (bf16[64,2560]{1,0:T(8,128)(2,1)}, bf16[64,1536]{1,0:T(8,128)(2,1)}, bf16[256,256]{1,0:T(8,128)(2,1)}, bf16[256,768]{1,0:T(8,128)(2,1)}) custom-call(bf16[512,2560]{1,0:T(8,128)(2,1)} %get-tuple-element.110.refs_0_.refs_2_, bf16[512,2560]{1,0:T(8,128)(2,1)} %get-tuple-element.111.refs_1_.refs_3_, bf16[256,2560]{1,0:T(8,128)(2,1)} %copy-done.1, ...), custom_call_target="tpu_custom_call" | custom-call | flops 6291456 | bytes 6291456 | tf_op jit(solution)/shard_map/combine/pallas_call | solution.py:99
  175.4 14.7 %wgrad.3 = (bf16[512,1536]{1,0:T(8,128)(2,1)}, bf16[512,1536]{1,0:T(8,128)(2,1)}, f32[1,1536]{1,0:T(1,128)}, bf16[64,2560]{1,0:T(8,128)(2,1)}, bf16[64,1536]{1,0...) custom-call(bf16[256,1024]{1,0:T(8,128)(2,1)} %get-tuple-element.105.refs_2_.refs_0_.refs_5_, ...), custom_call_target="tpu_custom_call" | custom-call | flops 4831838208 | bytes 11010048 | tf_op jit(solution)/shard_map/wgrad/pallas_call | solution.py:99
  190.1 2.8 combine.9
  192.9 29.9 %attention.5 = (bf16[512,512]{1,0:T(8,128)(2,1)}, bf16[1536,1536]{1,0:T(8,128)(2,1)}, bf16[32,2560]{1,0:T(8,128)(2,1)}, bf16[32,1536]{1,0:T(8,128)(2,1)}, bf16[1...) custom-call(s32[1,512]{1,0:T(1,128)} %bitcast.39, ...), custom_call_target="tpu_custom_call" | custom-call | flops 6442450944 | bytes 11010048 | tf_op jit(solution)/shard_map/attention/pallas_call | solution.py:99
  222.8 4.7 %combine.10 = (bf16[512,1536]{1,0:T(8,128)(2,1)}, f32[32,4096]{1,0:T(8,128)}, f32[128,1024]{1,0:T(8,128)}) custom-call(bf16[512,1536]{1,0:T(8,128)(2,1)} %get-tuple-element.160.refs_0_, bf16[512,1536]{1,0:T(8,128)(2,1)} %get-tuple-element.161.refs_1_, bf16[512,2560]{1,0:T(8,128)(2,1)} %get-tuple-element.110.refs_0_.refs_2_, ...), custom_call_target="tpu_custom_call" | custom-call | flops 10485760 | bytes 10485760 | tf_op jit(solution)/shard_map/combine/pallas_call | solution.py:99
  227.5 90.2 %tail.1 = (bf16[512,1024]{1,0:T(8,128)(2,1)}, f32[512,1024]{1,0:T(8,128)}, f32[16,1024]{1,0:T(8,128)}, f32[32,1536]{1,0:T(8,128)}, f32[32,1536]{1,0:T(8,128)}, /...) custom-call(bf16[1536,768]{1,0:T(8,128)(2,1)} %get-tuple-element.125, ...), custom_call_target="tpu_custom_call" | custom-call | flops 32212254720 | bytes 20971520 | tf_op jit(solution)/shard_map/tail/pallas_call | solution.py:1041
  317.7 0.0 copy-start.3
  317.7 0.9 slice_bitcast_fusion
  318.6 0.8 slice.37
  319.4 1.0 fusion.14
  320.3 0.1 fusion.7
  320.4 0.0 copy-start.6
  320.4 0.6 fusion.3
  321.0 0.6 fusion.4
  321.6 0.6 fusion.5
  322.2 0.6 fusion.6
  322.8 0.6 dynamic_slice.42
  323.3 0.6 dynamic_slice.39
  323.9 2.2 combine.11
  326.1 0.5 copy.37
  326.6 2.3 copy.38
  328.9 0.0 copy-done.3
  328.9 1.3 copy.39
  330.2 0.0 copy-done.6
  (6 shorter events, 0.0 us)
Async XLA Ops:
  92.8 43.5 %collective-permute-start.3 = (bf16[1024,768]{1,0:T(8,128)(2,1)}, bf16[1024,768]{1,0:T(8,128)(2,1)S(1)}, u32[]{:S(2)}, u32[]{:S(2)}) collective-permute-start(bf16[1024,768]{1,0:T(8,128)(2,1)} %get-tuple-element.128), channel_id=1, source_target_pairs={{0,1},{1,0},{2,3},{3,2},{4,5},{5,4},{6,7},{7,6},{8,9},{9,8},{10,11... | collective-permute-start | bytes 4718600 | tf_op jit(solution)/shard_map/ppermute | solution.py:204
  93.9 42.5 %collective-permute-start = (bf16[256,2560]{1,0:T(8,128)(2,1)}, bf16[256,2560]{1,0:T(8,128)(2,1)S(1)}, u32[]{:S(2)}, u32[]{:S(2)}) collective-permute-start(bf16[256,2560]{1,0:T(8,128)(2,1)} %get-tuple-element.121.refs_8_), channel_id=1, source_target_pairs={{0,8},{4,12},{8,0},{12,4},{16,24},{20,28},{24,16},{28,20},{1,9},{5... | collective-permute-start | bytes 3932168 | tf_op jit(solution)/shard_map/ppermute | solution.py:204
  95.3 41.0 %collective-permute-start.1 = (bf16[256,1536]{1,0:T(8,128)(2,1)}, bf16[256,1536]{1,0:T(8,128)(2,1)}, u32[]{:S(2)}, u32[]{:S(2)}) collective-permute-start(bf16[256,1536]{1,0:T(8,128)(2,1)} %get-tuple-element.126), channel_id=1, source_target_pairs={{0,16},{4,20},{8,24},{12,28},{16,0},{20,4},{24,8},{28,12},{1,17},{... | collective-permute-start | bytes 2359304 | tf_op jit(solution)/shard_map/ppermute | solution.py:204
  96.9 39.5 %collective-permute-start.2 = (bf16[1024,256]{1,0:T(8,128)(2,1)}, bf16[1024,256]{1,0:T(8,128)(2,1)S(1)}, u32[]{:S(2)}, u32[]{:S(2)}) collective-permute-start(bf16[1024,256]{1,0:T(8,128)(2,1)} %get-tuple-element.127), channel_id=1, source_target_pairs={{0,16},{4,20},{8,24},{12,28},{16,0},{20,4},{24,8},{28,12},{1,17},{... | collective-permute-start | bytes 1572872 | tf_op jit(solution)/shard_map/ppermute | solution.py:204
  101.9 17.9 %copy-start.4 = (f32[1024]{0:T(1024)S(1)}, f32[1024]{0:T(1024)}, u32[]{:S(2)}) copy-start(f32[1024]{0:T(1024)} %param.24) | copy-start | bytes 12292
  101.9 17.9 %copy-start.5 = (f32[1024]{0:T(1024)S(1)}, f32[1024]{0:T(1024)}, u32[]{:S(2)}) copy-start(f32[1024]{0:T(1024)} %param.28) | copy-start | bytes 12292
  136.3 0.8 copy-start.2
  136.3 1.2 copy-start.1
  136.4 1.7 copy-start
  317.7 11.2 %copy-start.3 = (f32[512,1024]{1,0:T(8,128)S(1)}, f32[512,1024]{1,0:T(8,128)}, u32[]{:S(2)}) copy-start(f32[512,1024]{1,0:T(8,128)} %get-tuple-element.168) | copy-start | bytes 6291460
  320.4 9.8 %copy-start.6 = (f32[32]{0:T(128)}, f32[32]{0:T(128)S(1)}, u32[]{:S(2)}) copy-start(f32[32]{0:T(128)S(1)} %fusion.7) | copy-start | bytes 388
where the time goes:
time: 335 us; the launch traced here: 330 us
  Pallas kernels  304 us (91%)
  local copies, waits for them, and re-layouts  13.5 us (4%)
  other arithmetic  7.07 us (2%)
  starting transfers between devices  4.53 us (1%)
    pallas_call x16, Pallas kernels, call(): pl.pallas_call(body, grid_spec=pltpu.PrefetchScalarGridSpec(num_scalar_pr...  214 us
    pallas_call x1, Pallas kernels, tail(): pl.pallas_call(body, grid_spec=pltpu.PrefetchScalarGridSpec(num_scalar_pr...  90.2 us
    unnamed x19, local copies, waits for them, and re-layouts  6.71 us
  transfers between devices with their start and end apart: 4, of which 0 were waited for; matrix products, arithmetic and copies ran while one was open for 2% of the time, Pallas kernels for 10%

commit v1 on v0

--- a/solution.py
+++ b/solution.py
@@ -160,7 +160,7 @@
 
 
 def combine(items, after=(), joined=()):
-    steps = 4 if all(rows % 64 == 0 for _, _, rows, _ in items) else 1
+    steps = 2 if all(rows % 32 == 0 for _, _, rows, _ in items) else 1
     ins, specs, counts, slots, shapes, nbytes = [], [], [], [], [], 0
     for k, (arrays, lo, rows, dtype) in enumerate(items):
         block, cols = rows // steps, arrays[0][0].shape[1]
@@ -190,6 +190,40 @@
     )
 
 
+def last_kernel(counts, nseq, *refs):
+    n = sum(counts)
+    small_ref, outs = refs[n], refs[n + 1 :]
+    combine_kernel(counts, [(0, 0), (0, refs[0].shape[1]), (1, 0)], *refs[:n], *outs[:2])
+    d = small_ref.shape[1]
+    me = lax.axis_index("dp") * nseq + lax.axis_index("seq")
+    lines = [(k, 1) for k in (0, 1, 2, 3, 4, 4)] + [(5, 3), (8, outs[-1].shape[1] * d // outs[2].shape[1] // d)]
+    for (at, rows), out in zip(lines, outs[2:]):
+        flat = jnp.concatenate([small_ref[at + r : at + r + 1, :] for r in range(rows)], axis=1)
+        flat = jnp.broadcast_to(flat, (8, rows * d))
+        mine = out.shape[1]
+        out[...] = pltpu.roll(flat, rows * d - me * mine, 1)[:1, :mine]
+
+
+def last_sums(terms, small, ff, ndev, nseq):
+    arrays = [a for term, *_ in terms for a, _ in term]
+    rows = terms[0][2]
+    d = small.shape[1]
+    widths = [term[0][0].shape[1] for term, *_ in terms]
+    shapes = [(rows, widths[0] + widths[1]), (rows, widths[2])] + [(1, d // ndev)] * 6 + [(1, 3 * d // ndev), (1, ff // ndev)]
+    return call(
+        functools.partial(last_kernel, [len(term) for term, *_ in terms], nseq),
+        *arrays,
+        small,
+        grid=(1,),
+        in_specs=[whole((rows, a.shape[1])) for a in arrays] + [whole(small.shape)],
+        out_specs=[whole(shape) for shape in shapes],
+        out_shape=[jax.ShapeDtypeStruct(shape, F32) for shape in shapes],
+        name="last",
+        flops=rows * d * 20,
+        nbytes=rows * d * 40,
+    )
+
+
 class Halving:
     def __init__(self, send, keep, stages, sizes):
         self.keep, self.stages, self.sizes = keep, list(stages), sizes
@@ -258,7 +292,7 @@
 
 def norms(x, dy, live, g1, b1, g2, b2, after=()):
     rows, d = x.shape
-    tr = 128
+    tr = min(256, rows)
     row = pl.BlockSpec((tr, d), lambda i: (i, 0))
     return call(
         norm_kernel,
@@ -296,7 +330,7 @@
 def mlp(m, grad, win, b_in, wout, after=(), sends=(), cid=None):
     rows, d = m.shape
     ff = win.shape[1]
-    tf = 512
+    tf = 1024
     cols = pl.BlockSpec((rows, tf), lambda i: (0, i))
     line = pl.BlockSpec((1, tf), lambda i: (0, i))
     return call(
@@ -756,8 +790,10 @@
     ndp, nseq, halos, n_pieces, n_dp, n_ctx, joins, last_c = cfg
     refs = list(refs)
     take = lambda n: [refs.pop(0) for _ in range(n)]
-    dp_rows, (w_ref,), dp_cols, pieces, ctxs = take(n_dp), take(1), take(n_dp - 2), take(n_pieces), take(n_ctx)
-    grad_ref, x_ref, mlp_ref, d_mlp_ref, wd_ref, bias_ref, g1, g2 = take(8)
+    dp_rows, (w_ref,) = take(n_dp), take(1)
+    n_late = n_dp - 2 + n_pieces + n_ctx + 3
+    late = take(n_late)
+    mlp_ref, wd_ref, bias_ref, g1, g2 = take(5)
     gsum_ref, qsum_ref, isum_ref = take(3)
     left_q, own_q = take(2)
     hidden_ref, grad_in_ref, small = take(3)
@@ -766,7 +802,14 @@
     nat, lt, own_acc, far, far_got = take(5)
     group_bufs = [take(6), take(6), [None, own_q.at[0], None, left_q, *take(2)]]
     bsum_ref, small_got = take(2)
-    send_sem, recv_sem = refs
+    held = take(n_late)
+    send_sem, recv_sem, late_sem = refs
+    loads = [pltpu.make_async_copy(a, b, late_sem.at[k]) for k, (a, b) in enumerate(zip(late, held))]
+    held = list(held)
+    take_held = lambda n: [held.pop(0) for _ in range(n)]
+    dp_cols, pieces, ctxs = take_held(n_dp - 2), take_held(n_pieces), take_held(n_ctx)
+    grad_ref, x_ref, d_mlp_ref = held
+    first_loads = n_dp - 2 + n_pieces
     toks, d = x_ref.shape
     me_dp, me_seq = lax.axis_index("dp"), lax.axis_index("seq")
     dp_bits = stage_bits(ndp)
@@ -791,7 +834,12 @@
             device_id_type=pl.DeviceIdType.MESH,
         )
 
-    far_copy = lambda k: copy(("far", k), far.at[k], far_got.at[k], behind)
+    half = toks // 2
+
+    def far_copy(k, c):
+        rows = pl.ds(c * half, half)
+        return copy(("far", k, c), far.at[k, rows], far_got.at[k, rows], behind)
+
 
     def first(n):
         send, _, got, *_ = group_bufs[n]
@@ -835,16 +883,17 @@
             else:
                 own[...] = total
 
-    def pass_on(k):
-        far_copy(k - 1).wait()
-        far[k] = (far[k].astype(F32) + far_got[k - 1].astype(F32)).astype(BF16)
-        far_copy(k).start()
-
-    def back(cols=None):
+    def pass_on(k, c):
+        far_copy(k - 1, c).wait()
+        rows = pl.ds(c * half, half)
+        far[k, rows] = (far[k, rows].astype(F32) + far_got[k - 1, rows].astype(F32)).astype(BF16)
+        far_copy(k, c).start()
+
+    def back(rows=slice(None)):
         total, at = None, 0
         for a_ref in dp_rows:
             n = a_ref.shape[1]
-            term = dot_t(a_ref[...], w_ref[:, at : at + n])
+            term = dot_t(a_ref[rows, :], w_ref[:, at : at + n])
             total, at = term if total is None else total + term, at + n
         return total
 
@@ -861,15 +910,19 @@
             if k == 0:
                 offsets = [("dp", o) for o in (*core[1:], *cross[1:])] + [("seq", o) for o in across[1:]]
                 greet([device(*o) for o in offsets] + [behind, ahead])
-                for c in second(2):
+                for c in loads + second(2):
                     c.start()
-            far[k] = back().astype(BF16)
-            if k == 0:
-                far_copy(0).start()
+            for c in range(2):
+                rows = slice(c * half, (c + 1) * half)
+                far[k, rows] = back(rows).astype(BF16)
+                if k == 0:
+                    far_copy(0, c).start()
 
         phase(do_far)
 
     def do_columns():
+        for c in loads[:first_loads]:
+            c.wait()
         col = 0
         for left in pieces:
             n = left.shape[0]
@@ -886,10 +939,14 @@
             bsum_ref[:, at : at + n] = jnp.sum(right.astype(F32), axis=0, keepdims=True)
             at += n
         first(0).start()
+        if halos > 1:
+            pass_on(1, 0)
 
     phase(do_columns)
 
     def do_dense():
+        for c in loads[first_loads:]:
+            c.wait()
         at = 0
         for ctx in ctxs:
             turned(ctx[...], nat, at)
@@ -907,6 +964,8 @@
 
     def do_own():
         own_acc[...] = back()
+        if halos > 1:
+            pass_on(1, 1)
         to_second(1)
 
     phase(do_own)
@@ -921,20 +980,20 @@
                 total += dot(ctx[...], wd_ref[row : row + n, :])
                 row += n
             hidden_ref[...] = total.astype(BF16)
-            if t == 0 and halos > 1:
-                pass_on(1)
 
         phase(do_join)
 
     def do_rest():
         for k in range(2, halos):
-            pass_on(k)
+            for c in range(2):
+                pass_on(k, c)
         to_third(0)
         to_third(1)
-        far_copy(halos - 1).wait()
         small[...] = jnp.zeros_like(small)
-        rows = min(128, toks)
+        rows = min(128, half)
         for r in range(0, toks, rows):
+            if r % half == 0:
+                far_copy(halos - 1, r // half).wait()
             at = slice(r, r + rows)
             u, inv = unit_of(x_ref[at, :].astype(F32))
             d1 = own_acc[at, :] + far_got[halos - 1, at, :].astype(F32)
@@ -984,15 +1043,13 @@
     hbm = pl.BlockSpec(memory_space=pl.ANY)
     cut_up = lambda a, n: a.reshape(n, a.shape[0] // n, a.shape[1])
     left_q = cut_up(left_q, cross)
-    ins = [*dps, w, *dps[2:], *pieces, *ctxs, grad, x, mlp_out, d_mlp, w_d, bias, g1, g2, *sums, left_q, left_q]
+    late = [*dps[2:], *pieces, *ctxs, grad, x, d_mlp]
+    ins = [*dps, w, *late, mlp_out, w_d, bias, g1, g2, *sums, left_q, left_q]
     in_specs = (
         [pl.BlockSpec((toks, a.shape[1]), piece_at) for a in dps]
         + [once(w.shape)]
-        + [once(a.shape) for a in dps[2:]]
-        + [once(p.shape) for p in pieces]
-        + [once(c.shape) for c in ctxs]
-        + [once((toks, d))] * 2
-        + [pl.BlockSpec((toks, tile), join_at), once((toks, d)), pl.BlockSpec((d, tile), join_at)]
+        + [hbm] * len(late)
+        + [pl.BlockSpec((toks, tile), join_at), pl.BlockSpec((d, tile), join_at)]
         + [once((1, d))] * 3
         + [once(v.shape) for v in sums]
         + [hbm, once((1, *left_q.shape[1:]))]
@@ -1030,8 +1087,9 @@
         scratch += [pltpu.VMEM((across - 1, left, n), kind)]
     scratch += [pltpu.VMEM((cross - 1, *left_q.shape[1:]), BF16), pltpu.VMEM((across - 1, left, widths[0]), kind)]
     scratch += [pltpu.VMEM((1, rest), F32), pltpu.VMEM((1 + cross - 1 + across - 1, lines, d), F32)]
-    copies = halos + 4 * (1 + cross - 1 + across - 1)
-    scratch += [pltpu.SemaphoreType.DMA((copies,))] * 2
+    scratch += [pltpu.VMEM(a.shape, a.dtype) for a in late]
+    copies = 2 * halos + 4 * (1 + cross - 1 + across - 1)
+    scratch += [pltpu.SemaphoreType.DMA((copies,))] * 2 + [pltpu.SemaphoreType.DMA((len(late),))]
     cfg = (ndp, nseq, halos, len(pieces), len(dps), len(ctxs), joins, seq_bits)
     n = len(ins)
 
@@ -1113,43 +1171,56 @@
 
     ahead = [(i, (i + 1) % nseq) for i in range(nseq)]
     on = ("ring", 1, nseq)
+    fine = toks // 4 % LANES == 0
+    cut = toks * 3 // 4 if fine else toks
     mlp_out, act, d_pre, d_mlp, b_in_sum, near = mlp(
-        m_own, grad, fc_in_weight, row(fc_in_bias), fc_out_weight, sends=[(a_own, 0, toks, on)], cid=2
-    )
-    pieces = [a_own, near]
+        m_own, grad, fc_in_weight, row(fc_in_bias), fc_out_weight, sends=[(a_own, 0, cut, on)], cid=2
+    )
+    near, far = [near], []
+    two = halos > 1
 
     orders = [stage_order(ndp, nseq, kind) for kind in range(3)]
     srcs = [(o, nseq) for o in orders]
     in_cut, out_cut = ff * 5 // 8, d // 4
-    hop = [[(near, k * toks // 2, toks // 2, on)] if halos > 1 else [] for k in range(2)]
-    s0, k0, _, s1, k1, _, *far_low = wgrad(
-        [(srcs[0], in_cut), (srcs[2], ff - in_cut)], [m_own], d_pre, sends=hop[0], cid=3 if hop[0] else None
-    )
+    sends = [(a_own, cut, toks - cut, on)] if fine else []
+    if two:
+        sends.append((near[0], 0, toks // 4 if fine else toks // 2, on))
+    s0, k0, line, s1, k1, _, *got = wgrad(
+        [(srcs[0], in_cut), (srcs[2], ff - in_cut)], [m_own], d_pre, sends=sends, cid=3 if sends else None
+    )
+    near += got[:1] if fine else []
+    far += got[-1:] if two else []
     early = [Halving(s0, k0, orders[0], sizes), Halving(s1, k1, orders[2], sizes)]
     s2, k2, s3, k3, *got = wgrad_rows(
         [(srcs[2], out_cut), (srcs[1], d - out_cut)],
         act,
         grad,
-        after=far_low,
-        sends=[send for r in early for send in r.sends()] + hop[1],
+        after=[line],
+        sends=[send for r in early for send in r.sends()]
+        + ([(near[0], far[0].shape[0], toks // 2, on)] if two else []),
         cid=4,
     )
     for r in early:
         r.receive([got.pop(0)])
-    if halos > 1:
-        pieces += [got[0], far_low[0]]
-    for k in range(2, halos):
-        after_two = jnp.concatenate([pieces[3], pieces[2]], axis=0) if k == 2 else pieces[-1]
-        pieces.append(lax.ppermute(after_two, "seq", ahead))
+    far += got
     late = [Halving(s2, k2, orders[2], sizes), Halving(s3, k3, orders[1], sizes)]
     fc = early + late
-    d_ctx, *got = d_context(grad, dense_weight, sends=[send for r in late for send in r.sends()], cid=5)
+    d_ctx, *got = d_context(
+        grad,
+        dense_weight,
+        sends=[send for r in late for send in r.sends()] + ([(near[1], 0, toks - cut, on)] if two and fine else []),
+        cid=5,
+    )
     for r in late:
         r.receive([got.pop(0)])
+    far += got
+    pieces = [*far, *near, a_own]
+    for k in range(2, halos):
+        far = [lax.ppermute(jnp.concatenate(far, axis=0), "seq", ahead)]
+        pieces = far + pieces
     last = advance(fc, [d_ctx])
     for r in fc:
         r.permute()
-    pieces = pieces[::-1]
     q, k, v = qkv(pieces, qkv_weight, row(qkv_bias), cos, sin, after=last)
 
     order_c = short_order(ndp, nseq)
@@ -1203,12 +1274,8 @@
         halos,
     )
     hidden_out, grad_in, small = main
-    g_qkv, g_dense = combine(terms, joined=(1,))
-    mine = lambda lo, rows: lax.dynamic_slice_in_dim(
-        small[lo : lo + rows].reshape(-1), (me_dp * nseq + me_seq) * (rows * d // ndev), rows * d // ndev
-    )
-    o1g, o1b, o2g, o2b, o_db = (mine(k, 1) for k in range(5))
-    o_qb, o_ib = mine(5, 3), mine(8, ff // d)
+    g_qkv, g_dense, *parts = last_sums(terms, small, ff, ndev, nseq)
+    o1g, o1b, o2g, o2b, o_db, o_ob, o_qb, o_ib = (v.reshape(-1) for v in parts)
     return (
         hidden_out.reshape(hidden_in.shape),
         grad_in.reshape(hidden_in.shape),
@@ -1223,7 +1290,7 @@
         g_in,
         o_ib,
         g_out,
-        o_db,
+        o_ob,
     )
 
 

time: 335 us -> 321 us (0.958)
  Pallas kernels: 304 us -> 297 us
  local copies, waits for them, and re-layouts: 13.5 us -> 6.98 us
    pallas_call x1, Pallas kernels: 90.2 us -> 84.7 us  [tail(): pl.pallas_call(body, grid_spec=pltpu.PrefetchScalarGridSpec(num_scalar_pr...]
    dynamic_slice x7 -> x0, local copies, waits for them, and re-layouts: 3.57 us -> none  [shards(): lax.dynamic_slice_in_dim(small[lo:lo + rows].reshape(-1), (me_dp * nseq +...]
    unnamed x19 -> x16, local copies, waits for them, and re-layouts: 6.71 us -> 5.54 us
  transfers between devices with their start and end apart: 4 -> 4, of which waited for: 0 -> 0; matrix products, arithmetic and copies ran while one was open for 2% -> 2% of each run, Pallas kernels for 10% -> 11%
where the time goes in v1:
time: 321 us; the launch traced here: 316 us
  Pallas kernels  297 us (93%)
  other arithmetic  7.1 us (2%)
  local copies, waits for them, and re-layouts  6.98 us (2%)
  starting transfers between devices  4.4 us (1%)
    pallas_call x16, Pallas kernels, call(): pl.pallas_call(body, grid_spec=pltpu.PrefetchScalarGridSpec(num_scalar_pr...  212 us
    pallas_call x1, Pallas kernels, tail(): pl.pallas_call(body, grid_spec=pltpu.PrefetchScalarGridSpec(num_scalar_pr...  84.7 us
  transfers between devices with their start and end apart: 4, of which 0 were waited for; matrix products, arithmetic and copies ran while one was open for 2% of the time, Pallas kernels for 11%

profile of v1, /device:TPU:0, one launch (start us, length us, event | category | flops | bytes accessed | tf_op | source)
XLA Modules:
  0.0 316.1 jit_solution(14027440903005609821)
XLA Ops:
  0.7 0.8 select_reduce_fusion.1
  1.4 0.6 slice.11
  2.0 0.6 fusion.2
  2.7 0.9 copy.30.refs_2_
  3.5 3.7 %norms.1 = (bf16[512,1024]{1,0:T(8,128)(2,1)}, bf16[512,1024]{1,0:T(8,128)(2,1)}, bf16[512,1024]{1,0:T(8,128)(2,1)}, f32[1,1024]{1,0:T(1,128)}) custom-call(bf16[512,1024]{1,0:T(8,128)(2,1)} %bitcast.26, bf16[512,1024]{1,0:T(8,128)(2,1)} %bitcast.25, f32[512,1]{1,0:T(8,128)} %copy.30.refs_2_, f32[1,1024]{1,0:T(1,128)} %bitcast.35, f32[1,1024]{1,0:T(1,128)} %bitcast.33, ...), custom_call_target="tpu_custom_call" | custom-call | flops 10485760 | bytes 5242880 | tf_op jit(solution)/shard_map/norms/pallas_call | solution.py:99
  7.3 30.8 %mlp.1 = (f32[512,1024]{1,0:T(8,128)}, bf16[512,4096]{1,0:T(8,128)(2,1)}, bf16[512,4096]{1,0:T(8,128)(2,1)}, f32[512,1024]{1,0:T(8,128)}, f32[1,4096]{1,0:T(1,128)}, /*index=5*/bf16[384,1024]{1,0:T(8,128)(2,1)}) custom-call(bf16[512,1024]{1,0:T(8,128)(2,1)} %get-tuple-element.111.refs_0_, bf16[512,1024]{1,0:T(8,128)(2,1)} %get-tuple-element.112.refs_1_.refs_0_.refs_14_, ...), custom_call_target="tpu_custom_call" | custom-call | flops 17179869184 | bytes 31457280 | tf_op jit(solution)/shard_map/mlp/pallas_call | solution.py:99
  38.0 18.5 %wgrad.2 = (bf16[512,2560]{1,0:T(8,128)(2,1)}, bf16[512,2560]{1,0:T(8,128)(2,1)}, f32[1,2560]{1,0:T(1,128)}, bf16[512,1536]{1,0:T(8,128)(2,1)}, bf16[512,1536]{1...) custom-call(bf16[512,1024]{1,0:T(8,128)(2,1)} %get-tuple-element.111.refs_0_, ...), custom_call_target="tpu_custom_call" | custom-call | flops 4294967296 | bytes 13631488 | tf_op jit(solution)/shard_map/wgrad/pallas_call | solution.py:99
  56.5 18.3 %wgrad_rows.1 = (bf16[2048,256]{1,0:T(8,128)(2,1)}, bf16[2048,256]{1,0:T(8,128)(2,1)}, bf16[2048,768]{1,0:T(8,128)(2,1)}, bf16[2048,768]{1,0:T(8,128)(2,1)}, bf1...) custom-call(bf16[512,4096]{1,0:T(8,128)(2,1)} %get-tuple-element.117.refs_0_, ...), custom_call_target="tpu_custom_call" | custom-call | flops 4294967296 | bytes 13631488 | tf_op jit(solution)/shard_map/wgrad_rows/pallas_call | solution.py:99
  74.8 10.7 %d_ctx.1 = (bf16[512,1024]{1,0:T(8,128)(2,1)}, bf16[2048,256]{1,0:T(8,128)(2,1)}, bf16[2048,768]{1,0:T(8,128)(2,1)}, bf16[128,1024]{1,0:T(8,128)(2,1)}) custom-call(bf16[512,1024]{1,0:T(8,128)(2,1)} %get-tuple-element.112.refs_1_.refs_0_.refs_14_, bf16[1024,1024]{1,0:T(8,128)(2,1)} %refs_18_.1, bf16[2048,256]{1,0:T(8,128)(2,1)} %get-tuple-element.122.refs_2_, ...), custom_call_target="tpu_custom_call" | custom-call | flops 1073741824 | bytes 4194304 | tf_op jit(solution)/shard_map/d_ctx/pallas_call | solution.py:99
  85.6 5.2 %combine.5 = (bf16[256,2560]{1,0:T(8,128)(2,1)}, bf16[256,1536]{1,0:T(8,128)(2,1)}, bf16[1024,256]{1,0:T(8,128)(2,1)}, bf16[1024,768]{1,0:T(8,128)(2,1)}) custom-call(bf16[512,2560]{1,0:T(8,128)(2,1)} %get-tuple-element.126.refs_0_.refs_2_, bf16[512,2560]{1,0:T(8,128)(2,1)} %get-tuple-element.127.refs_1_.refs_3_, ...), custom_call_target="tpu_custom_call" | custom-call | flops 16777216 | bytes 16777216 | tf_op jit(solution)/shard_map/combine/pallas_call | solution.py:99
  90.7 0.9 collective-permute-start.3
  91.6 1.5 collective-permute-start
  93.1 1.5 collective-permute-start.1
  94.6 0.5 collective-permute-start.2
  95.1 0.1 select_reduce_fusion
  95.3 4.4 %fusion.1 = (f32[1536,128]{1,0:T(8,128)}, f32[1536,128]{1,0:T(8,128)}) fusion(f32[128]{0:T(128)S(1)} %get-tuple-element.210, f32[128]{0:T(128)S(1)} %get-tuple-element.211, f32[1536]{0:T(1024)S(1)} %subtract_convert_fusion, pred[128]{0:T(512)(128)(4,1)S(1)} %broadcast_compare_fusion), kind=kLoop, calls=%fused_computation.3 | loop fusion | flops 589824 | bytes 1580160 | tf_op jit(solution)/shard_map/mul | solution.py:1165
  99.7 0.0 copy-start.5
  99.7 0.0 copy-start.6
  99.7 18.4 %qkv.1 = (bf16[512,1024]{1,0:T(8,128)(2,1)}, bf16[1536,1024]{1,0:T(8,128)(2,1)}, bf16[1536,1024]{1,0:T(8,128)(2,1)}) custom-call(bf16[128,1024]{1,0:T(8,128)(2,1)} %get-tuple-element.116.refs_0_.refs_5_, bf16[256,1024]{1,0:T(8,128)(2,1)} %get-tuple-element.121.refs_1_.refs_6_, bf16[128,1024]{1,0:T(8,128)(2,1)} %get-tuple-element.125.refs_2_.refs_7_, ...), custom_call_target="tpu_custom_call" | custom-call | flops 9663676416 | bytes 18874368 | tf_op jit(solution)/shard_map/qkv/pallas_call | solution.py:99
  118.0 0.0 copy-done.5
  118.1 0.0 copy-done.6
  118.1 0.6 add.46
  118.7 0.6 slice_subtract_fusion
  119.2 15.4 %attention.3 = (bf16[512,256]{1,0:T(8,128)(2,1)}, bf16[1536,768]{1,0:T(8,128)(2,1)}) custom-call(s32[1,512]{1,0:T(1,128)} %bitcast.29, bf16[512,1024]{1,0:T(8,128)(2,1)} %get-tuple-element.136.refs_1_, bf16[1536,1024]{1,0:T(8,128)(2,1)} %get-tuple-element.137.refs_2_, bf16[1536,1024]{1,0:T(8,128)(2,1)} %get-tuple-element.138.refs_3_, ...), custom_call_target="tpu_custom_call" | custom-call | flops 3221225472 | bytes 5505024 | tf_op jit(solution)/shard_map/attention/pallas_call | solution.py:99
  134.6 0.0 collective-permute-done.2.refs_8_.refs_10_.refs_12_.refs_16_
  134.6 0.0 copy-start.3
  134.6 0.0 collective-permute-done.1.refs_5_.refs_6_.refs_7_.refs_10_
  134.6 0.0 copy-start.2
  134.6 0.0 collective-permute-done.refs_2_.refs_4_
  134.7 0.0 copy-start.1
  134.7 0.0 collective-permute-done.3.refs_11_.refs_14_.refs_17_.refs_22_
  134.7 0.0 copy-start
  134.7 0.7 copy-done.3
  135.4 0.3 copy-done.2
  135.7 0.5 copy-done.1
  136.2 0.5 copy-done
  136.6 4.1 %combine.6 = (bf16[128,2560]{1,0:T(8,128)(2,1)}, bf16[128,1536]{1,0:T(8,128)(2,1)}, bf16[512,256]{1,0:T(8,128)(2,1)}, bf16[512,768]{1,0:T(8,128)(2,1)}) custom-call(bf16[512,2560]{1,0:T(8,128)(2,1)} %get-tuple-element.126.refs_0_.refs_2_, bf16[512,2560]{1,0:T(8,128)(2,1)} %get-tuple-element.127.refs_1_.refs_3_, bf16[256,2560]{1,0:T(8,128)(2,1)} %copy-done.1, ...), custom_call_target="tpu_custom_call" | custom-call | flops 10485760 | bytes 10485760 | tf_op jit(solution)/shard_map/combine/pallas_call | solution.py:99
  140.7 28.5 %attention.4 = (bf16[512,256]{1,0:T(8,128)(2,1)}, bf16[1536,768]{1,0:T(8,128)(2,1)}, bf16[128,2560]{1,0:T(8,128)(2,1)}, bf16[128,1536]{1,0:T(8,128)(2,1)}, bf16[...) custom-call(s32[1,512]{1,0:T(1,128)} %bitcast.30, bf16[512,1024]{1,0:T(8,128)(2,1)} %get-tuple-element.136.refs_1_, ...), custom_call_target="tpu_custom_call" | custom-call | flops 3221225472 | bytes 5505024 | tf_op jit(solution)/shard_map/attention/pallas_call | solution.py:99
  169.2 3.3 %combine.7 = (bf16[64,2560]{1,0:T(8,128)(2,1)}, bf16[64,1536]{1,0:T(8,128)(2,1)}, bf16[256,256]{1,0:T(8,128)(2,1)}, bf16[256,768]{1,0:T(8,128)(2,1)}) custom-call(bf16[512,2560]{1,0:T(8,128)(2,1)} %get-tuple-element.126.refs_0_.refs_2_, bf16[512,2560]{1,0:T(8,128)(2,1)} %get-tuple-element.127.refs_1_.refs_3_, bf16[256,2560]{1,0:T(8,128)(2,1)} %copy-done.1, ...), custom_call_target="tpu_custom_call" | custom-call | flops 6291456 | bytes 6291456 | tf_op jit(solution)/shard_map/combine/pallas_call | solution.py:99
  172.5 14.8 %wgrad.3 = (bf16[512,1536]{1,0:T(8,128)(2,1)}, bf16[512,1536]{1,0:T(8,128)(2,1)}, f32[1,1536]{1,0:T(1,128)}, bf16[64,2560]{1,0:T(8,128)(2,1)}, bf16[64,1536]{1,0...) custom-call(bf16[128,1024]{1,0:T(8,128)(2,1)} %get-tuple-element.116.refs_0_.refs_5_, ...), custom_call_target="tpu_custom_call" | custom-call | flops 4831838208 | bytes 11010048 | tf_op jit(solution)/shard_map/wgrad/pallas_call | solution.py:99
  187.3 2.7 combine.8
  190.0 30.9 %attention.5 = (bf16[512,512]{1,0:T(8,128)(2,1)}, bf16[1536,1536]{1,0:T(8,128)(2,1)}, bf16[32,2560]{1,0:T(8,128)(2,1)}, bf16[32,1536]{1,0:T(8,128)(2,1)}, bf16[1...) custom-call(s32[1,512]{1,0:T(1,128)} %bitcast.31, ...), custom_call_target="tpu_custom_call" | custom-call | flops 6442450944 | bytes 11010048 | tf_op jit(solution)/shard_map/attention/pallas_call | solution.py:99
  220.8 4.2 %combine.9 = (bf16[512,1536]{1,0:T(8,128)(2,1)}, f32[32,4096]{1,0:T(8,128)}, f32[128,1024]{1,0:T(8,128)}) custom-call(bf16[512,1536]{1,0:T(8,128)(2,1)} %get-tuple-element.174.refs_0_, bf16[512,1536]{1,0:T(8,128)(2,1)} %get-tuple-element.175.refs_1_, bf16[512,2560]{1,0:T(8,128)(2,1)} %get-tuple-element.126.refs_0_.refs_2_, ...), custom_call_target="tpu_custom_call" | custom-call | flops 10485760 | bytes 10485760 | tf_op jit(solution)/shard_map/combine/pallas_call | solution.py:99
  225.1 84.7 %tail.1 = (bf16[512,1024]{1,0:T(8,128)(2,1)}, f32[512,1024]{1,0:T(8,128)}, f32[16,1024]{1,0:T(8,128)}, f32[32,1536]{1,0:T(8,128)}, f32[32,1536]{1,0:T(8,128)}, /...) custom-call(bf16[1536,768]{1,0:T(8,128)(2,1)} %get-tuple-element.139, ...), custom_call_target="tpu_custom_call" | custom-call | flops 32212254720 | bytes 20971520 | tf_op jit(solution)/shard_map/tail/pallas_call | solution.py:1099
  309.8 0.0 copy-start.4
  309.8 2.5 last.1
  312.4 2.3 copy.33
  314.6 0.0 copy-done.4
  314.6 1.3 copy.34
  (4 shorter events, 0.0 us)
Async XLA Ops:
  90.7 44.0 %collective-permute-start.3 = (bf16[1024,768]{1,0:T(8,128)(2,1)}, bf16[1024,768]{1,0:T(8,128)(2,1)S(1)}, u32[]{:S(2)}, u32[]{:S(2)}) collective-permute-start(bf16[1024,768]{1,0:T(8,128)(2,1)} %get-tuple-element.142), channel_id=1, source_target_pairs={{0,1},{1,0},{2,3},{3,2},{4,5},{5,4},{6,7},{7,6},{8,9},{9,8},{10,11... | collective-permute-start | bytes 4718600 | tf_op jit(solution)/shard_map/ppermute | solution.py:238
  91.6 43.0 %collective-permute-start = (bf16[256,2560]{1,0:T(8,128)(2,1)}, bf16[256,2560]{1,0:T(8,128)(2,1)S(1)}, u32[]{:S(2)}, u32[]{:S(2)}) collective-permute-start(bf16[256,2560]{1,0:T(8,128)(2,1)} %get-tuple-element.135.refs_10_), channel_id=1, source_target_pairs={{0,8},{4,12},{8,0},{12,4},{16,24},{20,28},{24,16},{28,20},{1,9},{5... | collective-permute-start | bytes 3932168 | tf_op jit(solution)/shard_map/ppermute | solution.py:238
  93.1 41.5 %collective-permute-start.1 = (bf16[256,1536]{1,0:T(8,128)(2,1)}, bf16[256,1536]{1,0:T(8,128)(2,1)S(1)}, u32[]{:S(2)}, u32[]{:S(2)}) collective-permute-start(bf16[256,1536]{1,0:T(8,128)(2,1)} %get-tuple-element.140), channel_id=1, source_target_pairs={{0,16},{4,20},{8,24},{12,28},{16,0},{20,4},{24,8},{28,12},{1,17},{... | collective-permute-start | bytes 2359304 | tf_op jit(solution)/shard_map/ppermute | solution.py:238
  94.6 40.0 %collective-permute-start.2 = (bf16[1024,256]{1,0:T(8,128)(2,1)}, bf16[1024,256]{1,0:T(8,128)(2,1)S(1)}, u32[]{:S(2)}, u32[]{:S(2)}) collective-permute-start(bf16[1024,256]{1,0:T(8,128)(2,1)} %get-tuple-element.141), channel_id=1, source_target_pairs={{0,16},{4,20},{8,24},{12,28},{16,0},{20,4},{24,8},{28,12},{1,17},{... | collective-permute-start | bytes 1572872 | tf_op jit(solution)/shard_map/ppermute | solution.py:238
  99.7 18.4 %copy-start.5 = (f32[1024]{0:T(1024)S(1)}, f32[1024]{0:T(1024)}, u32[]{:S(2)}) copy-start(f32[1024]{0:T(1024)} %param.24) | copy-start | bytes 12292
  99.7 18.4 %copy-start.6 = (f32[1024]{0:T(1024)S(1)}, f32[1024]{0:T(1024)}, u32[]{:S(2)}) copy-start(f32[1024]{0:T(1024)} %param.28) | copy-start | bytes 12292
  134.6 0.8 copy-start.3
  134.6 1.1 copy-start.2
  134.7 1.5 copy-start.1
  134.7 1.9 copy-start
  309.8 4.8 %copy-start.4 = (f32[512,1024]{1,0:T(8,128)S(1)}, f32[512,1024]{1,0:T(8,128)}, u32[]{:S(2)}) copy-start(f32[512,1024]{1,0:T(8,128)} %get-tuple-element.182) | copy-start | bytes 6291460

commit v2 on v1

--- a/solution.py
+++ b/solution.py
@@ -276,11 +276,15 @@
     return c * inv, inv
 
 
-def norm_kernel(x_ref, dy_ref, live_ref, g1, b1, g2, b2, a_ref, m_ref, grad_ref, sum_ref):
+def norm_kernel(len_ref, x_ref, dy_ref, g1, b1, g2, b2, a_ref, m_ref, grad_ref, sum_ref):
     u, _ = unit_of(x_ref[...].astype(F32))
     a_ref[...] = (u * g1[...] + b1[...]).astype(BF16)
     m_ref[...] = (u * g2[...] + b2[...]).astype(BF16)
-    grad = dy_ref[...].astype(F32) * live_ref[...]
+    rows = x_ref.shape[0]
+    toks = rows * pl.num_programs(0)
+    at = lax.axis_index("seq") * toks + pl.program_id(0) * rows + lax.broadcasted_iota(jnp.int32, (rows, 1), 0)
+    text = sum(len_ref[k] for k in range(len_ref.shape[0] - 1))
+    grad = dy_ref[...].astype(F32) * jnp.where(at < text, 1.0, 0.0)
     grad_ref[...] = grad.astype(BF16)
 
     @pl.when(pl.program_id(0) == 0)
@@ -290,15 +294,22 @@
     sum_ref[...] += jnp.sum(grad, axis=0, keepdims=True)
 
 
-def norms(x, dy, live, g1, b1, g2, b2, after=()):
+def norms(lengths, x, dy, g1, b1, g2, b2, after=()):
     rows, d = x.shape
     tr = min(256, rows)
-    row = pl.BlockSpec((tr, d), lambda i: (i, 0))
+    row = pl.BlockSpec((tr, d), lambda i, *_: (i, 0))
     return call(
         norm_kernel,
-        x, dy, live, g1, b1, g2, b2,
+        lengths,
+        x,
+        dy,
+        g1,
+        b1,
+        g2,
+        b2,
+        scalars=1,
         grid=(rows // tr,),
-        in_specs=[row, row, pl.BlockSpec((tr, 1), lambda i: (i, 0))] + [whole((1, d))] * 4,
+        in_specs=[row, row] + [whole((1, d))] * 4,
         out_specs=[row, row, row, whole((1, d))],
         out_shape=[jax.ShapeDtypeStruct((rows, d), BF16)] * 3 + [jax.ShapeDtypeStruct((1, d), F32)],
         flops=rows * d * 20, nbytes=rows * d * 10,
@@ -521,20 +532,55 @@
     )
 
 
-def d_ctx_kernel(a_ref, w_ref, out_ref):
+def document_start(len_ref, at):
+    begin, end = jnp.zeros_like(at), 0
+    for k in range(len_ref.shape[0]):
+        end = end + len_ref[k]
+        begin = jnp.where(at >= end, end, begin)
+    return begin
+
+
+def d_ctx_kernel(halos, nseq, len_ref, a_ref, w_ref, out_ref, cos_ref, sin_ref, start_ref):
     out_ref[...] = dot_t(a_ref[...], w_ref[...]).astype(BF16)
-
-
-def d_context(grad, w, tn=256, after=(), sends=(), cid=None):
+    toks, rows = a_ref.shape[0], cos_ref.shape[0]
+    me = lax.axis_index("seq")
+    base = (me - halos) * toks
+    at = base + pl.program_id(0) * rows + lax.broadcasted_iota(jnp.int32, (rows, LANES), 0)
+    lane = lane_ids(rows) % HEAD
+    half = ROT // 2
+    freq = jnp.zeros((rows, LANES), F32)
+    for k in range(half):
+        freq = jnp.where(lane % half == k, 10000.0 ** (-(2.0 * k) / ROT), freq)
+    angle = (at - document_start(len_ref, at)).astype(F32) * freq
+    cos_ref[...] = jnp.where(lane < ROT, jnp.cos(angle), 1.0)
+    sin = jnp.sin(angle)
+    sin_ref[...] = jnp.where(lane < half, -sin, jnp.where(lane < ROT, sin, 0.0))
+    own = me * toks + lax.broadcasted_iota(jnp.int32, (1, toks), 1)
+    start_ref[...] = document_start(len_ref, own) - base
+
+
+def d_context(lengths, grad, w, halos, nseq, tn=256, after=(), sends=(), cid=None):
     rows, d = grad.shape
+    win = rows * (halos + 1)
+    steps = d // tn
+    table = pl.BlockSpec((win // steps, LANES), lambda i, *_: (i, 0))
     return call(
-        d_ctx_kernel,
-        grad, w,
-        grid=(d // tn,),
-        in_specs=[whole((rows, d)), pl.BlockSpec((tn, d), lambda i: (i, 0))],
-        out_specs=[pl.BlockSpec((rows, tn), lambda i: (0, i))],
-        out_shape=[jax.ShapeDtypeStruct((rows, d), BF16)],
-        flops=2 * rows * d * d, nbytes=2 * d * (2 * rows + d),
+        functools.partial(d_ctx_kernel, halos, nseq),
+        lengths,
+        grad,
+        w,
+        scalars=1,
+        grid=(steps,),
+        in_specs=[whole((rows, d)), pl.BlockSpec((tn, d), lambda i, *_: (i, 0))],
+        out_specs=[pl.BlockSpec((rows, tn), lambda i, *_: (0, i)), table, table, whole((1, rows))],
+        out_shape=[
+            jax.ShapeDtypeStruct((rows, d), BF16),
+            jax.ShapeDtypeStruct((win, LANES), F32),
+            jax.ShapeDtypeStruct((win, LANES), F32),
+            jax.ShapeDtypeStruct((1, rows), jnp.int32),
+        ],
+        flops=2 * rows * d * d,
+        nbytes=2 * d * (2 * rows + d),
         name="d_ctx",
         after=after,
         sends=sends,
@@ -958,7 +1004,6 @@
         first(1).start()
         keep[...] = dot(lt[:half, :toks], grad_ref[...]).astype(BF16)
         to_second(0)
-        to_third(2)
 
     phase(do_dense)
 
@@ -987,13 +1032,14 @@
         for k in range(2, halos):
             for c in range(2):
                 pass_on(k, c)
-        to_third(0)
-        to_third(1)
         small[...] = jnp.zeros_like(small)
         rows = min(128, half)
         for r in range(0, toks, rows):
             if r % half == 0:
                 far_copy(halos - 1, r // half).wait()
+                if r == 0:
+                    for n in (2, 0, 1):
+                        to_third(n)
             at = slice(r, r + rows)
             u, inv = unit_of(x_ref[at, :].astype(F32))
             d1 = own_acc[at, :] + far_got[halos - 1, at, :].astype(F32)
@@ -1144,29 +1190,11 @@
     me_dp, me_seq = lax.axis_index("dp"), lax.axis_index("seq")
     row = lambda v: v.reshape(1, -1)
 
-    halos = min(-(-(DOC_MOST - 1) // toks), nseq - 1)
-    halos = max(halos, 1)
-    win = (halos + 1) * toks
-    base = (me_seq - halos) * toks
+    halos = max(min(-(-(DOC_MOST - 1) // toks), nseq - 1), 1)
     lengths = doc_lengths.reshape(-1)
-    docs = lengths.shape[0]
-    doc = jnp.arange(docs, dtype=jnp.int32)
-    ends = jnp.sum(jnp.where(doc[None, :] <= doc[:, None], lengths[None, :], 0), axis=1)
-    at = base + jnp.arange(win, dtype=jnp.int32)
-    begin = jnp.max(jnp.where(at[:, None] >= ends[None, :], ends[None, :], 0), axis=1)
-    doc_pos = at - begin
-    live = (at[halos * toks :] < ends[docs - 2]).astype(F32).reshape(toks, 1)
-    start = (begin - base)[halos * toks :]
-    lane = jnp.arange(LANES, dtype=jnp.int32) % HEAD
-    half = ROT // 2
-    freq = 10000.0 ** (-(2.0 * (lane % half).astype(F32)) / ROT)
-    angle = doc_pos.astype(F32)[:, None] * freq[None, :]
-    cos = jnp.where(lane < ROT, jnp.cos(angle), 1.0)
-    sin = jnp.where(lane < half, -1.0, jnp.where(lane < ROT, 1.0, 0.0)) * jnp.sin(angle)
-
     x = hidden_in.reshape(toks, d)
     a_own, m_own, grad, grad_sum = norms(
-        x, out_grad.reshape(toks, d), live, row(ln1_gain), row(ln1_bias), row(ln2_gain), row(ln2_bias)
+        lengths, x, out_grad.reshape(toks, d), row(ln1_gain), row(ln1_bias), row(ln2_gain), row(ln2_bias)
     )
 
     ahead = [(i, (i + 1) % nseq) for i in range(nseq)]
@@ -1205,9 +1233,12 @@
     far += got
     late = [Halving(s2, k2, orders[2], sizes), Halving(s3, k3, orders[1], sizes)]
     fc = early + late
-    d_ctx, *got = d_context(
+    d_ctx, cos, sin, start, *got = d_context(
+        lengths,
         grad,
         dense_weight,
+        halos,
+        nseq,
         sends=[send for r in late for send in r.sends()] + ([(near[1], 0, toks - cut, on)] if two and fine else []),
         cid=5,
     )
@@ -1231,7 +1262,7 @@
     def part(at, n, sums=(), **more):
         sends = [send for r in sums for send in r.sends()]
         ctx, dp, *got = attention(
-            row(start), q, k, v, d_ctx, cos, sin, at * quarter, n * quarter, sends=sends, cid=6 + at if sends else None, **more
+            start, q, k, v, d_ctx, cos, sin, at * quarter, n * quarter, sends=sends, cid=6 + at if sends else None, **more
         )
         for r in sums:
             r.receive([got.pop(0) for _ in r.targets()])

time: 321 us -> 315 us (0.981)
  other arithmetic: 7.1 us -> 0.59 us
    mul x1 -> x0, other arithmetic: 4.4 us -> none  [shards(): jnp.where(lane < half, -1.0, jnp.where(lane < ROT, 1.0, 0.0))]
  transfers between devices with their start and end apart: 4 -> 4, of which waited for: 0 -> 0; matrix products, arithmetic and copies ran while one was open for 2% -> 0% of each run, Pallas kernels for 11% -> 11%
where the time goes in v2:
time: 315 us; the launch traced here: 309 us
  Pallas kernels  298 us (95%)
  local copies, waits for them, and re-layouts  5.54 us (2%)
  starting transfers between devices  4.41 us (1%)
    pallas_call x16, Pallas kernels, call(): pl.pallas_call(body, grid_spec=pltpu.PrefetchScalarGridSpec(num_scalar_pr...  213 us
    pallas_call x1, Pallas kernels, tail(): pl.pallas_call(body, grid_spec=pltpu.PrefetchScalarGridSpec(num_scalar_pr...  84.7 us
  transfers between devices with their start and end apart: 4, of which 0 were waited for; matrix products, arithmetic and copies ran while one was open for 0% of the time, Pallas kernels for 11%

profile of v2, /device:TPU:0, one launch (start us, length us, event | category | flops | bytes accessed | tf_op | source)
XLA Modules:
  0.0 309.5 jit_solution(64152795641904561)
XLA Ops:
  0.6 4.5 %norms.1 = (bf16[512,1024]{1,0:T(8,128)(2,1)}, bf16[512,1024]{1,0:T(8,128)(2,1)}, bf16[512,1024]{1,0:T(8,128)(2,1)}, f32[1,1024]{1,0:T(1,128)}) custom-call(s32[8]{0:T(128)} %bitcast.33, bf16[512,1024]{1,0:T(8,128)(2,1)} %bitcast.23, bf16[512,1024]{1,0:T(8,128)(2,1)} %bitcast.22, f32[1,1024]{1,0:T(1,128)} %bitcast.28, f32[1,1024]{1,0:T(1,128)} %bitcast.26, ...), custom_call_target="tpu_custom_call" | custom-call | flops 10485760 | bytes 5242880 | tf_op jit(solution)/shard_map/norms/pallas_call | solution.py:99
  5.1 30.8 %mlp.1 = (f32[512,1024]{1,0:T(8,128)}, bf16[512,4096]{1,0:T(8,128)(2,1)}, bf16[512,4096]{1,0:T(8,128)(2,1)}, f32[512,1024]{1,0:T(8,128)}, f32[1,4096]{1,0:T(1,128)}, /*index=5*/bf16[384,1024]{1,0:T(8,128)(2,1)}) custom-call(bf16[512,1024]{1,0:T(8,128)(2,1)} %get-tuple-element.115.refs_0_, bf16[512,1024]{1,0:T(8,128)(2,1)} %get-tuple-element.114.refs_1_.refs_14_, ...), custom_call_target="tpu_custom_call" | custom-call | flops 17179869184 | bytes 31457280 | tf_op jit(solution)/shard_map/mlp/pallas_call | solution.py:99
  35.9 18.4 %wgrad.2 = (bf16[512,2560]{1,0:T(8,128)(2,1)}, bf16[512,2560]{1,0:T(8,128)(2,1)}, f32[1,2560]{1,0:T(1,128)}, bf16[512,1536]{1,0:T(8,128)(2,1)}, bf16[512,1536]{1...) custom-call(bf16[512,1024]{1,0:T(8,128)(2,1)} %get-tuple-element.115.refs_0_, ...), custom_call_target="tpu_custom_call" | custom-call | flops 4294967296 | bytes 13631488 | tf_op jit(solution)/shard_map/wgrad/pallas_call | solution.py:99
  54.3 18.3 %wgrad_rows.1 = (bf16[2048,256]{1,0:T(8,128)(2,1)}, bf16[2048,256]{1,0:T(8,128)(2,1)}, bf16[2048,768]{1,0:T(8,128)(2,1)}, bf16[2048,768]{1,0:T(8,128)(2,1)}, bf1...) custom-call(bf16[512,4096]{1,0:T(8,128)(2,1)} %get-tuple-element.117.refs_0_, ...), custom_call_target="tpu_custom_call" | custom-call | flops 4294967296 | bytes 13631488 | tf_op jit(solution)/shard_map/wgrad_rows/pallas_call | solution.py:99
  72.5 11.5 %d_ctx.1 = (bf16[512,1024]{1,0:T(8,128)(2,1)}, f32[1536,128]{1,0:T(8,128)}, f32[1536,128]{1,0:T(8,128)}, s32[1,512]{1,0:T(1,128)}, bf16[2048,256]{1,0:T(8,128)(2...) custom-call(s32[8]{0:T(128)} %bitcast.34, bf16[512,1024]{1,0:T(8,128)(2,1)} %get-tuple-element.114.refs_1_.refs_14_, ...), custom_call_target="tpu_custom_call" | custom-call | flops 1073741824 | bytes 4194304 | tf_op jit(solution)/shard_map/d_ctx/pallas_call | solution.py:99
  84.0 5.2 %combine.5 = (bf16[256,2560]{1,0:T(8,128)(2,1)}, bf16[256,1536]{1,0:T(8,128)(2,1)}, bf16[1024,256]{1,0:T(8,128)(2,1)}, bf16[1024,768]{1,0:T(8,128)(2,1)}) custom-call(bf16[512,2560]{1,0:T(8,128)(2,1)} %get-tuple-element.132.refs_0_.refs_2_, bf16[512,2560]{1,0:T(8,128)(2,1)} %get-tuple-element.133.refs_1_.refs_3_, ...), custom_call_target="tpu_custom_call" | custom-call | flops 16777216 | bytes 16777216 | tf_op jit(solution)/shard_map/combine/pallas_call | solution.py:99
  89.2 0.9 collective-permute-start.3
  90.1 1.5 collective-permute-start
  91.6 1.5 collective-permute-start.1
  93.1 0.5 collective-permute-start.2
  93.6 0.0 copy-start.5
  93.6 0.0 copy-start.6
  93.6 18.4 %qkv.1 = (bf16[512,1024]{1,0:T(8,128)(2,1)}, bf16[1536,1024]{1,0:T(8,128)(2,1)}, bf16[1536,1024]{1,0:T(8,128)(2,1)}) custom-call(bf16[128,1024]{1,0:T(8,128)(2,1)} %get-tuple-element.127.refs_0_.refs_5_, bf16[256,1024]{1,0:T(8,128)(2,1)} %get-tuple-element.128.refs_1_.refs_6_, bf16[128,1024]{1,0:T(8,128)(2,1)} %get-tuple-element.129.refs_2_.refs_7_, ...), custom_call_target="tpu_custom_call" | custom-call | flops 9663676416 | bytes 18874368 | tf_op jit(solution)/shard_map/qkv/pallas_call | solution.py:99
  112.0 0.0 copy-done.5
  112.0 0.0 copy-done.6
  112.0 0.6 add.3
  112.6 15.4 %attention.3 = (bf16[512,256]{1,0:T(8,128)(2,1)}, bf16[1536,768]{1,0:T(8,128)(2,1)}) custom-call(s32[1,512]{1,0:T(1,128)} %get-tuple-element.126.refs_0_, bf16[512,1024]{1,0:T(8,128)(2,1)} %get-tuple-element.142.refs_1_, bf16[1536,1024]{1,0:T(8,128)(2,1)} %get-tuple-element.143.refs_2_, bf16[1536,1024]{1,0:T(8,128)(2,1)} %get-tuple-element.144.refs_3_, ...), custom_call_target="tpu_custom_call" | custom-call | flops 3221225472 | bytes 5505024 | tf_op jit(solution)/shard_map/attention/pallas_call | solution.py:99
  128.0 0.0 collective-permute-done.2.refs_8_.refs_10_.refs_12_.refs_16_
  128.0 0.0 copy-start.3
  128.0 0.0 collective-permute-done.1.refs_5_.refs_6_.refs_7_.refs_10_
  128.0 0.0 copy-start.2
  128.0 0.0 collective-permute-done.refs_2_.refs_4_
  128.1 0.0 copy-start.1
  128.1 0.0 collective-permute-done.3.refs_11_.refs_14_.refs_17_.refs_22_
  128.1 0.0 copy-start
  128.1 0.7 copy-done.3
  128.8 0.3 copy-done.2
  129.1 0.4 copy-done.1
  129.5 0.5 copy-done
  130.0 4.1 %combine.6 = (bf16[128,2560]{1,0:T(8,128)(2,1)}, bf16[128,1536]{1,0:T(8,128)(2,1)}, bf16[512,256]{1,0:T(8,128)(2,1)}, bf16[512,768]{1,0:T(8,128)(2,1)}) custom-call(bf16[512,2560]{1,0:T(8,128)(2,1)} %get-tuple-element.132.refs_0_.refs_2_, bf16[512,2560]{1,0:T(8,128)(2,1)} %get-tuple-element.133.refs_1_.refs_3_, bf16[256,2560]{1,0:T(8,128)(2,1)} %copy-done.1, ...), custom_call_target="tpu_custom_call" | custom-call | flops 10485760 | bytes 10485760 | tf_op jit(solution)/shard_map/combine/pallas_call | solution.py:99
  134.1 28.5 %attention.4 = (bf16[512,256]{1,0:T(8,128)(2,1)}, bf16[1536,768]{1,0:T(8,128)(2,1)}, bf16[128,2560]{1,0:T(8,128)(2,1)}, bf16[128,1536]{1,0:T(8,128)(2,1)}, bf16[...) custom-call(s32[1,512]{1,0:T(1,128)} %get-tuple-element.126.refs_0_, bf16[512,1024]{1,0:T(8,128)(2,1)} %get-tuple-element.142.refs_1_, ...), custom_call_target="tpu_custom_call" | custom-call | flops 3221225472 | bytes 5505024 | tf_op jit(solution)/shard_map/attention/pallas_call | solution.py:99
  162.6 3.3 %combine.7 = (bf16[64,2560]{1,0:T(8,128)(2,1)}, bf16[64,1536]{1,0:T(8,128)(2,1)}, bf16[256,256]{1,0:T(8,128)(2,1)}, bf16[256,768]{1,0:T(8,128)(2,1)}) custom-call(bf16[512,2560]{1,0:T(8,128)(2,1)} %get-tuple-element.132.refs_0_.refs_2_, bf16[512,2560]{1,0:T(8,128)(2,1)} %get-tuple-element.133.refs_1_.refs_3_, bf16[256,2560]{1,0:T(8,128)(2,1)} %copy-done.1, ...), custom_call_target="tpu_custom_call" | custom-call | flops 6291456 | bytes 6291456 | tf_op jit(solution)/shard_map/combine/pallas_call | solution.py:99
  165.9 14.8 %wgrad.3 = (bf16[512,1536]{1,0:T(8,128)(2,1)}, bf16[512,1536]{1,0:T(8,128)(2,1)}, f32[1,1536]{1,0:T(1,128)}, bf16[64,2560]{1,0:T(8,128)(2,1)}, bf16[64,1536]{1,0...) custom-call(bf16[128,1024]{1,0:T(8,128)(2,1)} %get-tuple-element.127.refs_0_.refs_5_, ...), custom_call_target="tpu_custom_call" | custom-call | flops 4831838208 | bytes 11010048 | tf_op jit(solution)/shard_map/wgrad/pallas_call | solution.py:99
  180.7 2.7 combine.8
  183.4 30.9 %attention.5 = (bf16[512,512]{1,0:T(8,128)(2,1)}, bf16[1536,1536]{1,0:T(8,128)(2,1)}, bf16[32,2560]{1,0:T(8,128)(2,1)}, bf16[32,1536]{1,0:T(8,128)(2,1)}, bf16[1...) custom-call(s32[1,512]{1,0:T(1,128)} %get-tuple-element.126.refs_0_, ...), custom_call_target="tpu_custom_call" | custom-call | flops 6442450944 | bytes 11010048 | tf_op jit(solution)/shard_map/attention/pallas_call | solution.py:99
  214.2 4.2 %combine.9 = (bf16[512,1536]{1,0:T(8,128)(2,1)}, f32[32,4096]{1,0:T(8,128)}, f32[128,1024]{1,0:T(8,128)}) custom-call(bf16[512,1536]{1,0:T(8,128)(2,1)} %get-tuple-element.180.refs_0_, bf16[512,1536]{1,0:T(8,128)(2,1)} %get-tuple-element.181.refs_1_, bf16[512,2560]{1,0:T(8,128)(2,1)} %get-tuple-element.132.refs_0_.refs_2_, ...), custom_call_target="tpu_custom_call" | custom-call | flops 10485760 | bytes 10485760 | tf_op jit(solution)/shard_map/combine/pallas_call | solution.py:99
  218.4 84.7 %tail.1 = (bf16[512,1024]{1,0:T(8,128)(2,1)}, f32[512,1024]{1,0:T(8,128)}, f32[16,1024]{1,0:T(8,128)}, f32[32,1536]{1,0:T(8,128)}, f32[32,1536]{1,0:T(8,128)}, /...) custom-call(bf16[1536,768]{1,0:T(8,128)(2,1)} %get-tuple-element.145, ...), custom_call_target="tpu_custom_call" | custom-call | flops 32212254720 | bytes 20971520 | tf_op jit(solution)/shard_map/tail/pallas_call | solution.py:1145
  303.2 0.0 copy-start.4
  303.2 2.5 last.1
  305.7 2.3 copy.31
  308.0 0.0 copy-done.4
  308.0 1.3 copy.32
Async XLA Ops:
  89.2 38.9 %collective-permute-start.3 = (bf16[1024,768]{1,0:T(8,128)(2,1)}, bf16[1024,768]{1,0:T(8,128)(2,1)S(1)}, u32[]{:S(2)}, u32[]{:S(2)}) collective-permute-start(bf16[1024,768]{1,0:T(8,128)(2,1)} %get-tuple-element.148), channel_id=1, source_target_pairs={{0,1},{1,0},{2,3},{3,2},{4,5},{5,4},{6,7},{7,6},{8,9},{9,8},{10,11... | collective-permute-start | bytes 4718600 | tf_op jit(solution)/shard_map/ppermute | solution.py:238
  90.1 38.0 %collective-permute-start = (bf16[256,2560]{1,0:T(8,128)(2,1)}, bf16[256,2560]{1,0:T(8,128)(2,1)S(1)}, u32[]{:S(2)}, u32[]{:S(2)}) collective-permute-start(bf16[256,2560]{1,0:T(8,128)(2,1)} %get-tuple-element.141.refs_10_), channel_id=1, source_target_pairs={{0,8},{4,12},{8,0},{12,4},{16,24},{20,28},{24,16},{28,20},{1,9},{5... | collective-permute-start | bytes 3932168 | tf_op jit(solution)/shard_map/ppermute | solution.py:238
  91.6 36.4 %collective-permute-start.1 = (bf16[256,1536]{1,0:T(8,128)(2,1)}, bf16[256,1536]{1,0:T(8,128)(2,1)S(1)}, u32[]{:S(2)}, u32[]{:S(2)}) collective-permute-start(bf16[256,1536]{1,0:T(8,128)(2,1)} %get-tuple-element.146), channel_id=1, source_target_pairs={{0,16},{4,20},{8,24},{12,28},{16,0},{20,4},{24,8},{28,12},{1,17},{... | collective-permute-start | bytes 2359304 | tf_op jit(solution)/shard_map/ppermute | solution.py:238
  93.1 34.9 %collective-permute-start.2 = (bf16[1024,256]{1,0:T(8,128)(2,1)}, bf16[1024,256]{1,0:T(8,128)(2,1)S(1)}, u32[]{:S(2)}, u32[]{:S(2)}) collective-permute-start(bf16[1024,256]{1,0:T(8,128)(2,1)} %get-tuple-element.147), channel_id=1, source_target_pairs={{0,16},{4,20},{8,24},{12,28},{16,0},{20,4},{24,8},{28,12},{1,17},{... | collective-permute-start | bytes 1572872 | tf_op jit(solution)/shard_map/ppermute | solution.py:238
  93.6 18.4 %copy-start.5 = (f32[1024]{0:T(1024)S(1)}, f32[1024]{0:T(1024)}, u32[]{:S(2)}) copy-start(f32[1024]{0:T(1024)} %param.24) | copy-start | bytes 12292
  93.6 18.4 %copy-start.6 = (f32[1024]{0:T(1024)S(1)}, f32[1024]{0:T(1024)}, u32[]{:S(2)}) copy-start(f32[1024]{0:T(1024)} %param.28) | copy-start | bytes 12292
  128.0 0.8 copy-start.3
  128.0 1.1 copy-start.2
  128.1 1.4 copy-start.1
  128.1 1.9 copy-start
  303.2 4.8 %copy-start.4 = (f32[512,1024]{1,0:T(8,128)S(1)}, f32[512,1024]{1,0:T(8,128)}, u32[]{:S(2)}) copy-start(f32[512,1024]{1,0:T(8,128)} %get-tuple-element.188) | copy-start | bytes 6291460

commit v3 on v2

--- a/solution.py
+++ b/solution.py
@@ -192,7 +192,8 @@
 
 def last_kernel(counts, nseq, *refs):
     n = sum(counts)
-    small_ref, outs = refs[n], refs[n + 1 :]
+    small_ref, done_ref, kept_ref, *outs = refs[n:]
+    kept_ref[...] = done_ref[...]
     combine_kernel(counts, [(0, 0), (0, refs[0].shape[1]), (1, 0)], *refs[:n], *outs[:2])
     d = small_ref.shape[1]
     me = lax.axis_index("dp") * nseq + lax.axis_index("seq")
@@ -204,7 +205,7 @@
         out[...] = pltpu.roll(flat, rows * d - me * mine, 1)[:1, :mine]
 
 
-def last_sums(terms, small, ff, ndev, nseq):
+def last_sums(terms, small, done, ff, ndev, nseq):
     arrays = [a for term, *_ in terms for a, _ in term]
     rows = terms[0][2]
     d = small.shape[1]
@@ -214,10 +215,11 @@
         functools.partial(last_kernel, [len(term) for term, *_ in terms], nseq),
         *arrays,
         small,
+        done,
         grid=(1,),
-        in_specs=[whole((rows, a.shape[1])) for a in arrays] + [whole(small.shape)],
-        out_specs=[whole(shape) for shape in shapes],
-        out_shape=[jax.ShapeDtypeStruct(shape, F32) for shape in shapes],
+        in_specs=[whole((rows, a.shape[1])) for a in arrays] + [whole(small.shape), whole(done.shape)],
+        out_specs=[whole(done.shape)] + [whole(shape) for shape in shapes],
+        out_shape=[jax.ShapeDtypeStruct(done.shape, done.dtype)] + [jax.ShapeDtypeStruct(shape, F32) for shape in shapes],
         name="last",
         flops=rows * d * 20,
         nbytes=rows * d * 40,
@@ -860,7 +862,7 @@
     me_dp, me_seq = lax.axis_index("dp"), lax.axis_index("seq")
     dp_bits = stage_bits(ndp)
     core, cross = fan(dp_bits[:1]), fan(dp_bits[1:])
-    across = fan(last_c)
+    across, everyone = fan(last_c), fan(dp_bits)
 
     def device(axis, offset):
         return (me_dp ^ offset, me_seq) if axis == "dp" else (me_dp, me_seq ^ offset)
@@ -954,7 +956,7 @@
 
         def do_far(k=k):
             if k == 0:
-                offsets = [("dp", o) for o in (*core[1:], *cross[1:])] + [("seq", o) for o in across[1:]]
+                offsets = [("dp", o) for o in everyone[1:]] + [("seq", o) for o in across[1:]]
                 greet([device(*o) for o in offsets] + [behind, ahead])
                 for c in loads + second(2):
                     c.start()
@@ -1012,6 +1014,7 @@
         if halos > 1:
             pass_on(1, 1)
         to_second(1)
+        to_third(2)
 
     phase(do_own)
     for t in range(joins):
@@ -1032,14 +1035,13 @@
         for k in range(2, halos):
             for c in range(2):
                 pass_on(k, c)
+        to_third(0)
+        to_third(1)
         small[...] = jnp.zeros_like(small)
         rows = min(128, half)
         for r in range(0, toks, rows):
             if r % half == 0:
                 far_copy(halos - 1, r // half).wait()
-                if r == 0:
-                    for n in (2, 0, 1):
-                        to_third(n)
             at = slice(r, r + rows)
             u, inv = unit_of(x_ref[at, :].astype(F32))
             d1 = own_acc[at, :] + far_got[halos - 1, at, :].astype(F32)
@@ -1057,7 +1059,7 @@
                 small[row : row + 1, :] = flat[:, c : c + d]
                 row += 1
         used = 0
-        for axis, offsets in (("dp", core), ("dp", cross), ("seq", across)):
+        for axis, offsets in (("dp", everyone), ("seq", across)):
             copies = []
             for o in offsets[1:]:
                 copies.append(copy(("small", used), small, small_got.at[used], device(axis, o)))
@@ -1132,9 +1134,9 @@
         scratch += [pltpu.VMEM((cross - 1, d // 2 // cross, n), BF16)] * 2
         scratch += [pltpu.VMEM((across - 1, left, n), kind)]
     scratch += [pltpu.VMEM((cross - 1, *left_q.shape[1:]), BF16), pltpu.VMEM((across - 1, left, widths[0]), kind)]
-    scratch += [pltpu.VMEM((1, rest), F32), pltpu.VMEM((1 + cross - 1 + across - 1, lines, d), F32)]
+    scratch += [pltpu.VMEM((1, rest), F32), pltpu.VMEM((ndp - 1 + across - 1, lines, d), F32)]
     scratch += [pltpu.VMEM(a.shape, a.dtype) for a in late]
-    copies = 2 * halos + 4 * (1 + cross - 1 + across - 1)
+    copies = 2 * halos + 3 * (1 + cross - 1 + across - 1) + (ndp - 1 + across - 1)
     scratch += [pltpu.SemaphoreType.DMA((copies,))] * 2 + [pltpu.SemaphoreType.DMA((len(late),))]
     cfg = (ndp, nseq, halos, len(pieces), len(dps), len(ctxs), joins, seq_bits)
     n = len(ins)
@@ -1305,7 +1307,7 @@
         halos,
     )
     hidden_out, grad_in, small = main
-    g_qkv, g_dense, *parts = last_sums(terms, small, ff, ndev, nseq)
+    hidden_out, g_qkv, g_dense, *parts = last_sums(terms, small, hidden_out, ff, ndev, nseq)
     o1g, o1b, o2g, o2b, o_db, o_ob, o_qb, o_ib = (v.reshape(-1) for v in parts)
     return (
         hidden_out.reshape(hidden_in.shape),

time: 315 us -> 313 us (level)
  no operation moved by 1% of the time
where the time goes in v3:
time: 313 us; the launch traced here: 308 us
  Pallas kernels  299 us (96%)
  starting transfers between devices  4.41 us (1%)
  local copies, waits for them, and re-layouts  3.28 us (1%)
    pallas_call x16, Pallas kernels, call(): pl.pallas_call(body, grid_spec=pltpu.PrefetchScalarGridSpec(num_scalar_pr...  214 us
    pallas_call x1, Pallas kernels, tail(): pl.pallas_call(body, grid_spec=pltpu.PrefetchScalarGridSpec(num_scalar_pr...  84.8 us
  transfers between devices with their start and end apart: 4, of which 0 were waited for; matrix products, arithmetic and copies ran while one was open for 0% of the time, Pallas kernels for 11%

profile of v3, /device:TPU:0, one launch (start us, length us, event | category | flops | bytes accessed | tf_op | source)
XLA Modules:
  0.0 308.1 jit_solution(6363511264168578402)
XLA Ops:
  0.6 4.5 %norms.1 = (bf16[512,1024]{1,0:T(8,128)(2,1)}, bf16[512,1024]{1,0:T(8,128)(2,1)}, bf16[512,1024]{1,0:T(8,128)(2,1)}, f32[1,1024]{1,0:T(1,128)}) custom-call(s32[8]{0:T(128)} %bitcast.32, bf16[512,1024]{1,0:T(8,128)(2,1)} %bitcast.23, bf16[512,1024]{1,0:T(8,128)(2,1)} %bitcast.22, f32[1,1024]{1,0:T(1,128)} %bitcast.27, f32[1,1024]{1,0:T(1,128)} %bitcast.25, ...), custom_call_target="tpu_custom_call" | custom-call | flops 10485760 | bytes 5242880 | tf_op jit(solution)/shard_map/norms/pallas_call | solution.py:99
  5.1 30.8 %mlp.1 = (f32[512,1024]{1,0:T(8,128)}, bf16[512,4096]{1,0:T(8,128)(2,1)}, bf16[512,4096]{1,0:T(8,128)(2,1)}, f32[512,1024]{1,0:T(8,128)}, f32[1,4096]{1,0:T(1,128)}, /*index=5*/bf16[384,1024]{1,0:T(8,128)(2,1)}) custom-call(bf16[512,1024]{1,0:T(8,128)(2,1)} %get-tuple-element.116.refs_0_, bf16[512,1024]{1,0:T(8,128)(2,1)} %get-tuple-element.115.refs_1_.refs_14_, ...), custom_call_target="tpu_custom_call" | custom-call | flops 17179869184 | bytes 31457280 | tf_op jit(solution)/shard_map/mlp/pallas_call | solution.py:99
  35.9 18.4 %wgrad.2 = (bf16[512,2560]{1,0:T(8,128)(2,1)}, bf16[512,2560]{1,0:T(8,128)(2,1)}, f32[1,2560]{1,0:T(1,128)}, bf16[512,1536]{1,0:T(8,128)(2,1)}, bf16[512,1536]{1...) custom-call(bf16[512,1024]{1,0:T(8,128)(2,1)} %get-tuple-element.116.refs_0_, ...), custom_call_target="tpu_custom_call" | custom-call | flops 4294967296 | bytes 13631488 | tf_op jit(solution)/shard_map/wgrad/pallas_call | solution.py:99
  54.3 18.3 %wgrad_rows.1 = (bf16[2048,256]{1,0:T(8,128)(2,1)}, bf16[2048,256]{1,0:T(8,128)(2,1)}, bf16[2048,768]{1,0:T(8,128)(2,1)}, bf16[2048,768]{1,0:T(8,128)(2,1)}, bf1...) custom-call(bf16[512,4096]{1,0:T(8,128)(2,1)} %get-tuple-element.118.refs_0_, ...), custom_call_target="tpu_custom_call" | custom-call | flops 4294967296 | bytes 13631488 | tf_op jit(solution)/shard_map/wgrad_rows/pallas_call | solution.py:99
  72.5 11.5 %d_ctx.1 = (bf16[512,1024]{1,0:T(8,128)(2,1)}, f32[1536,128]{1,0:T(8,128)}, f32[1536,128]{1,0:T(8,128)}, s32[1,512]{1,0:T(1,128)}, bf16[2048,256]{1,0:T(8,128)(2...) custom-call(s32[8]{0:T(128)} %bitcast.33, bf16[512,1024]{1,0:T(8,128)(2,1)} %get-tuple-element.115.refs_1_.refs_14_, ...), custom_call_target="tpu_custom_call" | custom-call | flops 1073741824 | bytes 4194304 | tf_op jit(solution)/shard_map/d_ctx/pallas_call | solution.py:99
  84.0 5.2 %combine.5 = (bf16[256,2560]{1,0:T(8,128)(2,1)}, bf16[256,1536]{1,0:T(8,128)(2,1)}, bf16[1024,256]{1,0:T(8,128)(2,1)}, bf16[1024,768]{1,0:T(8,128)(2,1)}) custom-call(bf16[512,2560]{1,0:T(8,128)(2,1)} %get-tuple-element.133.refs_0_.refs_2_, bf16[512,2560]{1,0:T(8,128)(2,1)} %get-tuple-element.134.refs_1_.refs_3_, ...), custom_call_target="tpu_custom_call" | custom-call | flops 16777216 | bytes 16777216 | tf_op jit(solution)/shard_map/combine/pallas_call | solution.py:99
  89.2 0.9 collective-permute-start.3
  90.1 1.5 collective-permute-start
  91.6 1.5 collective-permute-start.1
  93.1 0.5 collective-permute-start.2
  93.6 0.0 copy-start.5
  93.6 0.0 copy-start.6
  93.6 18.4 %qkv.1 = (bf16[512,1024]{1,0:T(8,128)(2,1)}, bf16[1536,1024]{1,0:T(8,128)(2,1)}, bf16[1536,1024]{1,0:T(8,128)(2,1)}) custom-call(bf16[128,1024]{1,0:T(8,128)(2,1)} %get-tuple-element.128.refs_0_.refs_5_, bf16[256,1024]{1,0:T(8,128)(2,1)} %get-tuple-element.129.refs_1_.refs_6_, bf16[128,1024]{1,0:T(8,128)(2,1)} %get-tuple-element.130.refs_2_.refs_7_, ...), custom_call_target="tpu_custom_call" | custom-call | flops 9663676416 | bytes 18874368 | tf_op jit(solution)/shard_map/qkv/pallas_call | solution.py:99
  112.0 0.0 copy-done.5
  112.0 0.0 copy-done.6
  112.0 0.6 add.3
  112.6 15.4 %attention.3 = (bf16[512,256]{1,0:T(8,128)(2,1)}, bf16[1536,768]{1,0:T(8,128)(2,1)}) custom-call(s32[1,512]{1,0:T(1,128)} %get-tuple-element.127.refs_0_, bf16[512,1024]{1,0:T(8,128)(2,1)} %get-tuple-element.143.refs_1_, bf16[1536,1024]{1,0:T(8,128)(2,1)} %get-tuple-element.144.refs_2_, bf16[1536,1024]{1,0:T(8,128)(2,1)} %get-tuple-element.145.refs_3_, ...), custom_call_target="tpu_custom_call" | custom-call | flops 3221225472 | bytes 5505024 | tf_op jit(solution)/shard_map/attention/pallas_call | solution.py:99
  128.0 0.0 collective-permute-done.2.refs_8_.refs_10_.refs_12_.refs_16_
  128.0 0.0 copy-start.3
  128.0 0.0 collective-permute-done.1.refs_5_.refs_6_.refs_7_.refs_10_
  128.0 0.0 copy-start.2
  128.0 0.0 collective-permute-done.refs_2_.refs_4_
  128.1 0.0 copy-start.1
  128.1 0.0 collective-permute-done.3.refs_11_.refs_14_.refs_17_.refs_22_
  128.1 0.0 copy-start
  128.1 0.7 copy-done.3
  128.8 0.3 copy-done.2
  129.1 0.4 copy-done.1
  129.5 0.5 copy-done
  130.0 4.1 %combine.6 = (bf16[128,2560]{1,0:T(8,128)(2,1)}, bf16[128,1536]{1,0:T(8,128)(2,1)}, bf16[512,256]{1,0:T(8,128)(2,1)}, bf16[512,768]{1,0:T(8,128)(2,1)}) custom-call(bf16[512,2560]{1,0:T(8,128)(2,1)} %get-tuple-element.133.refs_0_.refs_2_, bf16[512,2560]{1,0:T(8,128)(2,1)} %get-tuple-element.134.refs_1_.refs_3_, bf16[256,2560]{1,0:T(8,128)(2,1)} %copy-done.1, ...), custom_call_target="tpu_custom_call" | custom-call | flops 10485760 | bytes 10485760 | tf_op jit(solution)/shard_map/combine/pallas_call | solution.py:99
  134.1 28.5 %attention.4 = (bf16[512,256]{1,0:T(8,128)(2,1)}, bf16[1536,768]{1,0:T(8,128)(2,1)}, bf16[128,2560]{1,0:T(8,128)(2,1)}, bf16[128,1536]{1,0:T(8,128)(2,1)}, bf16[...) custom-call(s32[1,512]{1,0:T(1,128)} %get-tuple-element.127.refs_0_, bf16[512,1024]{1,0:T(8,128)(2,1)} %get-tuple-element.143.refs_1_, ...), custom_call_target="tpu_custom_call" | custom-call | flops 3221225472 | bytes 5505024 | tf_op jit(solution)/shard_map/attention/pallas_call | solution.py:99
  162.6 3.3 %combine.7 = (bf16[64,2560]{1,0:T(8,128)(2,1)}, bf16[64,1536]{1,0:T(8,128)(2,1)}, bf16[256,256]{1,0:T(8,128)(2,1)}, bf16[256,768]{1,0:T(8,128)(2,1)}) custom-call(bf16[512,2560]{1,0:T(8,128)(2,1)} %get-tuple-element.133.refs_0_.refs_2_, bf16[512,2560]{1,0:T(8,128)(2,1)} %get-tuple-element.134.refs_1_.refs_3_, bf16[256,2560]{1,0:T(8,128)(2,1)} %copy-done.1, ...), custom_call_target="tpu_custom_call" | custom-call | flops 6291456 | bytes 6291456 | tf_op jit(solution)/shard_map/combine/pallas_call | solution.py:99
  165.9 14.8 %wgrad.3 = (bf16[512,1536]{1,0:T(8,128)(2,1)}, bf16[512,1536]{1,0:T(8,128)(2,1)}, f32[1,1536]{1,0:T(1,128)}, bf16[64,2560]{1,0:T(8,128)(2,1)}, bf16[64,1536]{1,0...) custom-call(bf16[128,1024]{1,0:T(8,128)(2,1)} %get-tuple-element.128.refs_0_.refs_5_, ...), custom_call_target="tpu_custom_call" | custom-call | flops 4831838208 | bytes 11010048 | tf_op jit(solution)/shard_map/wgrad/pallas_call | solution.py:99
  180.7 2.7 combine.8
  183.4 30.9 %attention.5 = (bf16[512,512]{1,0:T(8,128)(2,1)}, bf16[1536,1536]{1,0:T(8,128)(2,1)}, bf16[32,2560]{1,0:T(8,128)(2,1)}, bf16[32,1536]{1,0:T(8,128)(2,1)}, bf16[1...) custom-call(s32[1,512]{1,0:T(1,128)} %get-tuple-element.127.refs_0_, ...), custom_call_target="tpu_custom_call" | custom-call | flops 6442450944 | bytes 11010048 | tf_op jit(solution)/shard_map/attention/pallas_call | solution.py:99
  214.2 4.2 %combine.9 = (bf16[512,1536]{1,0:T(8,128)(2,1)}, f32[32,4096]{1,0:T(8,128)}, f32[128,1024]{1,0:T(8,128)}) custom-call(bf16[512,1536]{1,0:T(8,128)(2,1)} %get-tuple-element.181.refs_0_, bf16[512,1536]{1,0:T(8,128)(2,1)} %get-tuple-element.182.refs_1_, bf16[512,2560]{1,0:T(8,128)(2,1)} %get-tuple-element.133.refs_0_.refs_2_, ...), custom_call_target="tpu_custom_call" | custom-call | flops 10485760 | bytes 10485760 | tf_op jit(solution)/shard_map/combine/pallas_call | solution.py:99
  218.4 84.8 %tail.1 = (bf16[512,1024]{1,0:T(8,128)(2,1)}, f32[512,1024]{1,0:T(8,128)}, f32[16,1024]{1,0:T(8,128)}, f32[32,1536]{1,0:T(8,128)}, f32[32,1536]{1,0:T(8,128)}, /...) custom-call(bf16[1536,768]{1,0:T(8,128)(2,1)} %get-tuple-element.146, ...), custom_call_target="tpu_custom_call" | custom-call | flops 32212254720 | bytes 20971520 | tf_op jit(solution)/shard_map/tail/pallas_call | solution.py:1147
  303.3 0.0 copy-start.4
  303.3 3.3 %last.1 = (bf16[512,1024]{1,0:T(8,128)(2,1)}, f32[32,3072]{1,0:T(8,128)}, f32[32,1024]{1,0:T(8,128)}, f32[1,32]{1,0:T(1,128)}, f32[1,32]{1,0:T(1,128)}, /*index=...) custom-call(f32[32,1536]{1,0:T(8,128)} %get-tuple-element.188.refs_0, ...), custom_call_target="tpu_custom_call" | custom-call | flops 655360 | bytes 1310720 | tf_op jit(solution)/shard_map/last/pallas_call | solution.py:99
  306.6 0.0 copy-done.4
  306.6 1.3 copy.30
Async XLA Ops:
  89.2 38.9 %collective-permute-start.3 = (bf16[1024,768]{1,0:T(8,128)(2,1)}, bf16[1024,768]{1,0:T(8,128)(2,1)S(1)}, u32[]{:S(2)}, u32[]{:S(2)}) collective-permute-start(bf16[1024,768]{1,0:T(8,128)(2,1)} %get-tuple-element.149), channel_id=1, source_target_pairs={{0,1},{1,0},{2,3},{3,2},{4,5},{5,4},{6,7},{7,6},{8,9},{9,8},{10,11... | collective-permute-start | bytes 4718600 | tf_op jit(solution)/shard_map/ppermute | solution.py:240
  90.1 38.0 %collective-permute-start = (bf16[256,2560]{1,0:T(8,128)(2,1)}, bf16[256,2560]{1,0:T(8,128)(2,1)S(1)}, u32[]{:S(2)}, u32[]{:S(2)}) collective-permute-start(bf16[256,2560]{1,0:T(8,128)(2,1)} %get-tuple-element.142.refs_10_), channel_id=1, source_target_pairs={{0,8},{4,12},{8,0},{12,4},{16,24},{20,28},{24,16},{28,20},{1,9},{5... | collective-permute-start | bytes 3932168 | tf_op jit(solution)/shard_map/ppermute | solution.py:240
  91.6 36.4 %collective-permute-start.1 = (bf16[256,1536]{1,0:T(8,128)(2,1)}, bf16[256,1536]{1,0:T(8,128)(2,1)S(1)}, u32[]{:S(2)}, u32[]{:S(2)}) collective-permute-start(bf16[256,1536]{1,0:T(8,128)(2,1)} %get-tuple-element.147), channel_id=1, source_target_pairs={{0,16},{4,20},{8,24},{12,28},{16,0},{20,4},{24,8},{28,12},{1,17},{... | collective-permute-start | bytes 2359304 | tf_op jit(solution)/shard_map/ppermute | solution.py:240
  93.1 34.9 %collective-permute-start.2 = (bf16[1024,256]{1,0:T(8,128)(2,1)}, bf16[1024,256]{1,0:T(8,128)(2,1)S(1)}, u32[]{:S(2)}, u32[]{:S(2)}) collective-permute-start(bf16[1024,256]{1,0:T(8,128)(2,1)} %get-tuple-element.148), channel_id=1, source_target_pairs={{0,16},{4,20},{8,24},{12,28},{16,0},{20,4},{24,8},{28,12},{1,17},{... | collective-permute-start | bytes 1572872 | tf_op jit(solution)/shard_map/ppermute | solution.py:240
  93.6 18.4 %copy-start.5 = (f32[1024]{0:T(1024)S(1)}, f32[1024]{0:T(1024)}, u32[]{:S(2)}) copy-start(f32[1024]{0:T(1024)} %param.24) | copy-start | bytes 12292
  93.6 18.4 %copy-start.6 = (f32[1024]{0:T(1024)S(1)}, f32[1024]{0:T(1024)}, u32[]{:S(2)}) copy-start(f32[1024]{0:T(1024)} %param.28) | copy-start | bytes 12292
  128.0 0.8 copy-start.3
  128.0 1.1 copy-start.2
  128.1 1.4 copy-start.1
  128.1 1.9 copy-start
  303.3 3.3 %copy-start.4 = (f32[512,1024]{1,0:T(8,128)S(1)}, f32[512,1024]{1,0:T(8,128)}, u32[]{:S(2)}) copy-start(f32[512,1024]{1,0:T(8,128)} %get-tuple-element.203) | copy-start | bytes 6291460

commit v4 on v3

--- a/solution.py
+++ b/solution.py
@@ -963,8 +963,10 @@
             for c in range(2):
                 rows = slice(c * half, (c + 1) * half)
                 far[k, rows] = back(rows).astype(BF16)
-                if k == 0:
+                if k == 0 and (c == 0 or halos == 1):
                     far_copy(0, c).start()
+            if k == 1:
+                far_copy(0, 1).start()
 
         phase(do_far)
 

time: 313 us -> 313 us (level)
  no operation moved by 1% of the time
where the time goes in v4:
time: 313 us; the launch traced here: 308 us
  Pallas kernels  299 us (96%)
  starting transfers between devices  4.41 us (1%)
  local copies, waits for them, and re-layouts  3.28 us (1%)
    pallas_call x16, Pallas kernels, call(): pl.pallas_call(body, grid_spec=pltpu.PrefetchScalarGridSpec(num_scalar_pr...  214 us
    pallas_call x1, Pallas kernels, tail(): pl.pallas_call(body, grid_spec=pltpu.PrefetchScalarGridSpec(num_scalar_pr...  84.8 us
  transfers between devices with their start and end apart: 4, of which 0 were waited for; matrix products, arithmetic and copies ran while one was open for 0% of the time, Pallas kernels for 11%

profile of v4, /device:TPU:0, one launch (start us, length us, event | category | flops | bytes accessed | tf_op | source)
XLA Modules:
  0.0 308.1 jit_solution(14635755336733173316)
XLA Ops:
  0.6 4.5 %norms.1 = (bf16[512,1024]{1,0:T(8,128)(2,1)}, bf16[512,1024]{1,0:T(8,128)(2,1)}, bf16[512,1024]{1,0:T(8,128)(2,1)}, f32[1,1024]{1,0:T(1,128)}) custom-call(s32[8]{0:T(128)} %bitcast.32, bf16[512,1024]{1,0:T(8,128)(2,1)} %bitcast.23, bf16[512,1024]{1,0:T(8,128)(2,1)} %bitcast.22, f32[1,1024]{1,0:T(1,128)} %bitcast.27, f32[1,1024]{1,0:T(1,128)} %bitcast.25, ...), custom_call_target="tpu_custom_call" | custom-call | flops 10485760 | bytes 5242880 | tf_op jit(solution)/shard_map/norms/pallas_call | solution.py:99
  5.1 30.8 %mlp.1 = (f32[512,1024]{1,0:T(8,128)}, bf16[512,4096]{1,0:T(8,128)(2,1)}, bf16[512,4096]{1,0:T(8,128)(2,1)}, f32[512,1024]{1,0:T(8,128)}, f32[1,4096]{1,0:T(1,128)}, /*index=5*/bf16[384,1024]{1,0:T(8,128)(2,1)}) custom-call(bf16[512,1024]{1,0:T(8,128)(2,1)} %get-tuple-element.116.refs_0_, bf16[512,1024]{1,0:T(8,128)(2,1)} %get-tuple-element.115.refs_1_.refs_14_, ...), custom_call_target="tpu_custom_call" | custom-call | flops 17179869184 | bytes 31457280 | tf_op jit(solution)/shard_map/mlp/pallas_call | solution.py:99
  35.9 18.4 %wgrad.2 = (bf16[512,2560]{1,0:T(8,128)(2,1)}, bf16[512,2560]{1,0:T(8,128)(2,1)}, f32[1,2560]{1,0:T(1,128)}, bf16[512,1536]{1,0:T(8,128)(2,1)}, bf16[512,1536]{1...) custom-call(bf16[512,1024]{1,0:T(8,128)(2,1)} %get-tuple-element.116.refs_0_, ...), custom_call_target="tpu_custom_call" | custom-call | flops 4294967296 | bytes 13631488 | tf_op jit(solution)/shard_map/wgrad/pallas_call | solution.py:99
  54.3 18.3 %wgrad_rows.1 = (bf16[2048,256]{1,0:T(8,128)(2,1)}, bf16[2048,256]{1,0:T(8,128)(2,1)}, bf16[2048,768]{1,0:T(8,128)(2,1)}, bf16[2048,768]{1,0:T(8,128)(2,1)}, bf1...) custom-call(bf16[512,4096]{1,0:T(8,128)(2,1)} %get-tuple-element.118.refs_0_, ...), custom_call_target="tpu_custom_call" | custom-call | flops 4294967296 | bytes 13631488 | tf_op jit(solution)/shard_map/wgrad_rows/pallas_call | solution.py:99
  72.5 11.5 %d_ctx.1 = (bf16[512,1024]{1,0:T(8,128)(2,1)}, f32[1536,128]{1,0:T(8,128)}, f32[1536,128]{1,0:T(8,128)}, s32[1,512]{1,0:T(1,128)}, bf16[2048,256]{1,0:T(8,128)(2...) custom-call(s32[8]{0:T(128)} %bitcast.33, bf16[512,1024]{1,0:T(8,128)(2,1)} %get-tuple-element.115.refs_1_.refs_14_, ...), custom_call_target="tpu_custom_call" | custom-call | flops 1073741824 | bytes 4194304 | tf_op jit(solution)/shard_map/d_ctx/pallas_call | solution.py:99
  84.0 5.2 %combine.5 = (bf16[256,2560]{1,0:T(8,128)(2,1)}, bf16[256,1536]{1,0:T(8,128)(2,1)}, bf16[1024,256]{1,0:T(8,128)(2,1)}, bf16[1024,768]{1,0:T(8,128)(2,1)}) custom-call(bf16[512,2560]{1,0:T(8,128)(2,1)} %get-tuple-element.133.refs_0_.refs_2_, bf16[512,2560]{1,0:T(8,128)(2,1)} %get-tuple-element.134.refs_1_.refs_3_, ...), custom_call_target="tpu_custom_call" | custom-call | flops 16777216 | bytes 16777216 | tf_op jit(solution)/shard_map/combine/pallas_call | solution.py:99
  89.2 0.9 collective-permute-start.3
  90.1 1.5 collective-permute-start
  91.6 1.5 collective-permute-start.1
  93.1 0.5 collective-permute-start.2
  93.6 0.0 copy-start.5
  93.6 0.0 copy-start.6
  93.6 18.4 %qkv.1 = (bf16[512,1024]{1,0:T(8,128)(2,1)}, bf16[1536,1024]{1,0:T(8,128)(2,1)}, bf16[1536,1024]{1,0:T(8,128)(2,1)}) custom-call(bf16[128,1024]{1,0:T(8,128)(2,1)} %get-tuple-element.128.refs_0_.refs_5_, bf16[256,1024]{1,0:T(8,128)(2,1)} %get-tuple-element.129.refs_1_.refs_6_, bf16[128,1024]{1,0:T(8,128)(2,1)} %get-tuple-element.130.refs_2_.refs_7_, ...), custom_call_target="tpu_custom_call" | custom-call | flops 9663676416 | bytes 18874368 | tf_op jit(solution)/shard_map/qkv/pallas_call | solution.py:99
  112.0 0.0 copy-done.5
  112.0 0.0 copy-done.6
  112.0 0.6 add.3
  112.6 15.4 %attention.3 = (bf16[512,256]{1,0:T(8,128)(2,1)}, bf16[1536,768]{1,0:T(8,128)(2,1)}) custom-call(s32[1,512]{1,0:T(1,128)} %get-tuple-element.127.refs_0_, bf16[512,1024]{1,0:T(8,128)(2,1)} %get-tuple-element.143.refs_1_, bf16[1536,1024]{1,0:T(8,128)(2,1)} %get-tuple-element.144.refs_2_, bf16[1536,1024]{1,0:T(8,128)(2,1)} %get-tuple-element.145.refs_3_, ...), custom_call_target="tpu_custom_call" | custom-call | flops 3221225472 | bytes 5505024 | tf_op jit(solution)/shard_map/attention/pallas_call | solution.py:99
  128.0 0.0 collective-permute-done.2.refs_8_.refs_10_.refs_12_.refs_16_
  128.0 0.0 copy-start.3
  128.0 0.0 collective-permute-done.1.refs_5_.refs_6_.refs_7_.refs_10_
  128.0 0.0 copy-start.2
  128.0 0.0 collective-permute-done.refs_2_.refs_4_
  128.1 0.0 copy-start.1
  128.1 0.0 collective-permute-done.3.refs_11_.refs_14_.refs_17_.refs_22_
  128.1 0.0 copy-start
  128.1 0.7 copy-done.3
  128.8 0.3 copy-done.2
  129.1 0.4 copy-done.1
  129.5 0.5 copy-done
  130.0 4.1 %combine.6 = (bf16[128,2560]{1,0:T(8,128)(2,1)}, bf16[128,1536]{1,0:T(8,128)(2,1)}, bf16[512,256]{1,0:T(8,128)(2,1)}, bf16[512,768]{1,0:T(8,128)(2,1)}) custom-call(bf16[512,2560]{1,0:T(8,128)(2,1)} %get-tuple-element.133.refs_0_.refs_2_, bf16[512,2560]{1,0:T(8,128)(2,1)} %get-tuple-element.134.refs_1_.refs_3_, bf16[256,2560]{1,0:T(8,128)(2,1)} %copy-done.1, ...), custom_call_target="tpu_custom_call" | custom-call | flops 10485760 | bytes 10485760 | tf_op jit(solution)/shard_map/combine/pallas_call | solution.py:99
  134.1 28.5 %attention.4 = (bf16[512,256]{1,0:T(8,128)(2,1)}, bf16[1536,768]{1,0:T(8,128)(2,1)}, bf16[128,2560]{1,0:T(8,128)(2,1)}, bf16[128,1536]{1,0:T(8,128)(2,1)}, bf16[...) custom-call(s32[1,512]{1,0:T(1,128)} %get-tuple-element.127.refs_0_, bf16[512,1024]{1,0:T(8,128)(2,1)} %get-tuple-element.143.refs_1_, ...), custom_call_target="tpu_custom_call" | custom-call | flops 3221225472 | bytes 5505024 | tf_op jit(solution)/shard_map/attention/pallas_call | solution.py:99
  162.6 3.3 %combine.7 = (bf16[64,2560]{1,0:T(8,128)(2,1)}, bf16[64,1536]{1,0:T(8,128)(2,1)}, bf16[256,256]{1,0:T(8,128)(2,1)}, bf16[256,768]{1,0:T(8,128)(2,1)}) custom-call(bf16[512,2560]{1,0:T(8,128)(2,1)} %get-tuple-element.133.refs_0_.refs_2_, bf16[512,2560]{1,0:T(8,128)(2,1)} %get-tuple-element.134.refs_1_.refs_3_, bf16[256,2560]{1,0:T(8,128)(2,1)} %copy-done.1, ...), custom_call_target="tpu_custom_call" | custom-call | flops 6291456 | bytes 6291456 | tf_op jit(solution)/shard_map/combine/pallas_call | solution.py:99
  165.9 14.8 %wgrad.3 = (bf16[512,1536]{1,0:T(8,128)(2,1)}, bf16[512,1536]{1,0:T(8,128)(2,1)}, f32[1,1536]{1,0:T(1,128)}, bf16[64,2560]{1,0:T(8,128)(2,1)}, bf16[64,1536]{1,0...) custom-call(bf16[128,1024]{1,0:T(8,128)(2,1)} %get-tuple-element.128.refs_0_.refs_5_, ...), custom_call_target="tpu_custom_call" | custom-call | flops 4831838208 | bytes 11010048 | tf_op jit(solution)/shard_map/wgrad/pallas_call | solution.py:99
  180.7 2.7 combine.8
  183.4 30.9 %attention.5 = (bf16[512,512]{1,0:T(8,128)(2,1)}, bf16[1536,1536]{1,0:T(8,128)(2,1)}, bf16[32,2560]{1,0:T(8,128)(2,1)}, bf16[32,1536]{1,0:T(8,128)(2,1)}, bf16[1...) custom-call(s32[1,512]{1,0:T(1,128)} %get-tuple-element.127.refs_0_, ...), custom_call_target="tpu_custom_call" | custom-call | flops 6442450944 | bytes 11010048 | tf_op jit(solution)/shard_map/attention/pallas_call | solution.py:99
  214.2 4.2 %combine.9 = (bf16[512,1536]{1,0:T(8,128)(2,1)}, f32[32,4096]{1,0:T(8,128)}, f32[128,1024]{1,0:T(8,128)}) custom-call(bf16[512,1536]{1,0:T(8,128)(2,1)} %get-tuple-element.181.refs_0_, bf16[512,1536]{1,0:T(8,128)(2,1)} %get-tuple-element.182.refs_1_, bf16[512,2560]{1,0:T(8,128)(2,1)} %get-tuple-element.133.refs_0_.refs_2_, ...), custom_call_target="tpu_custom_call" | custom-call | flops 10485760 | bytes 10485760 | tf_op jit(solution)/shard_map/combine/pallas_call | solution.py:99
  218.4 84.8 %tail.1 = (bf16[512,1024]{1,0:T(8,128)(2,1)}, f32[512,1024]{1,0:T(8,128)}, f32[16,1024]{1,0:T(8,128)}, f32[32,1536]{1,0:T(8,128)}, f32[32,1536]{1,0:T(8,128)}, /...) custom-call(bf16[1536,768]{1,0:T(8,128)(2,1)} %get-tuple-element.146, ...), custom_call_target="tpu_custom_call" | custom-call | flops 32212254720 | bytes 20971520 | tf_op jit(solution)/shard_map/tail/pallas_call | solution.py:1149
  303.3 0.0 copy-start.4
  303.3 3.3 %last.1 = (bf16[512,1024]{1,0:T(8,128)(2,1)}, f32[32,3072]{1,0:T(8,128)}, f32[32,1024]{1,0:T(8,128)}, f32[1,32]{1,0:T(1,128)}, f32[1,32]{1,0:T(1,128)}, /*index=...) custom-call(f32[32,1536]{1,0:T(8,128)} %get-tuple-element.188.refs_0, ...), custom_call_target="tpu_custom_call" | custom-call | flops 655360 | bytes 1310720 | tf_op jit(solution)/shard_map/last/pallas_call | solution.py:99
  306.6 0.0 copy-done.4
  306.6 1.3 copy.30
Async XLA Ops:
  89.2 38.9 %collective-permute-start.3 = (bf16[1024,768]{1,0:T(8,128)(2,1)}, bf16[1024,768]{1,0:T(8,128)(2,1)S(1)}, u32[]{:S(2)}, u32[]{:S(2)}) collective-permute-start(bf16[1024,768]{1,0:T(8,128)(2,1)} %get-tuple-element.149), channel_id=1, source_target_pairs={{0,1},{1,0},{2,3},{3,2},{4,5},{5,4},{6,7},{7,6},{8,9},{9,8},{10,11... | collective-permute-start | bytes 4718600 | tf_op jit(solution)/shard_map/ppermute | solution.py:240
  90.1 38.0 %collective-permute-start = (bf16[256,2560]{1,0:T(8,128)(2,1)}, bf16[256,2560]{1,0:T(8,128)(2,1)S(1)}, u32[]{:S(2)}, u32[]{:S(2)}) collective-permute-start(bf16[256,2560]{1,0:T(8,128)(2,1)} %get-tuple-element.142.refs_10_), channel_id=1, source_target_pairs={{0,8},{4,12},{8,0},{12,4},{16,24},{20,28},{24,16},{28,20},{1,9},{5... | collective-permute-start | bytes 3932168 | tf_op jit(solution)/shard_map/ppermute | solution.py:240
  91.6 36.4 %collective-permute-start.1 = (bf16[256,1536]{1,0:T(8,128)(2,1)}, bf16[256,1536]{1,0:T(8,128)(2,1)S(1)}, u32[]{:S(2)}, u32[]{:S(2)}) collective-permute-start(bf16[256,1536]{1,0:T(8,128)(2,1)} %get-tuple-element.147), channel_id=1, source_target_pairs={{0,16},{4,20},{8,24},{12,28},{16,0},{20,4},{24,8},{28,12},{1,17},{... | collective-permute-start | bytes 2359304 | tf_op jit(solution)/shard_map/ppermute | solution.py:240
  93.1 34.9 %collective-permute-start.2 = (bf16[1024,256]{1,0:T(8,128)(2,1)}, bf16[1024,256]{1,0:T(8,128)(2,1)S(1)}, u32[]{:S(2)}, u32[]{:S(2)}) collective-permute-start(bf16[1024,256]{1,0:T(8,128)(2,1)} %get-tuple-element.148), channel_id=1, source_target_pairs={{0,16},{4,20},{8,24},{12,28},{16,0},{20,4},{24,8},{28,12},{1,17},{... | collective-permute-start | bytes 1572872 | tf_op jit(solution)/shard_map/ppermute | solution.py:240
  93.6 18.4 %copy-start.5 = (f32[1024]{0:T(1024)S(1)}, f32[1024]{0:T(1024)}, u32[]{:S(2)}) copy-start(f32[1024]{0:T(1024)} %param.24) | copy-start | bytes 12292
  93.6 18.4 %copy-start.6 = (f32[1024]{0:T(1024)S(1)}, f32[1024]{0:T(1024)}, u32[]{:S(2)}) copy-start(f32[1024]{0:T(1024)} %param.28) | copy-start | bytes 12292
  128.0 0.8 copy-start.3
  128.0 1.1 copy-start.2
  128.1 1.4 copy-start.1
  128.1 1.9 copy-start
  303.3 3.3 %copy-start.4 = (f32[512,1024]{1,0:T(8,128)S(1)}, f32[512,1024]{1,0:T(8,128)}, u32[]{:S(2)}) copy-start(f32[512,1024]{1,0:T(8,128)} %get-tuple-element.203) | copy-start | bytes 6291460
